TPU v7x, 32 devices: a whole 2x2x4 slice. The times are simulated.
32 devices in a mesh: groups: 2 (over y), tr: 8 (over z, x), tc: 2 (over core).
Axes of the slice: x: 2, y: 2, z: 4, core: 2. Of those that a mesh axis runs over, the one named last changes fastest.
Arguments:
- shift_plane: float32 [2, 8192, 4096], P(None, ('groups', 'tr'), 'tc'), parts along dimension 1, may hold values from -0.2 to 0.2
- height: float32 [8192, 4096], P(('groups', 'tr'), 'tc'), parts along dimension 0, may hold values from -4 to 4
- dipole: float32 [8192, 4096], P(('groups', 'tr'), 'tc'), parts along dimension 0, may hold values from -6 to 6
Outputs:
- velocity_update: float32 [3, 8192, 4096], P(None, ('groups', 'tr'), 'tc'), parts along dimension 1
- dipole_update: float32 [8192, 4096], P(('groups', 'tr'), 'tc'), parts along dimension 0
There are 2 independent parts, one for each index of `groups`. A program takes and returns all parts, laid end to end along the dimension named above; each array names one. Nothing has to cross between parts.
All inputs are finite; a program needn't handle non-finite values.
Results may differ from a plain program's by a relative error of at most 0.00009.
Values sent between devices are 32-bit elements; how exact they have to be, the bound alone decides.
A program may use at most 256 MiB of HBM per device.

v0:
```python
import math

import jax
import jax.numpy as jnp
from jax import lax
from jax.sharding import PartitionSpec as P

largest_wavenumber = lax.Precision.HIGHEST


def padded_2(x, sides, width):
    for axis, dim in sides:
        devices, length = (lax.axis_size(axis), x.shape[dim])
        up = [(i, (i + 1) % devices) for i in range(devices)]
        down = [(j, i) for i, j in up]
        last = lax.slice_in_dim(x, length - width, length, axis=dim)
        initial = lax.slice_in_dim(x, 0, width, axis=dim)
        before = lax.ppermute(last, axis, up)
        after = lax.ppermute(initial, axis, down)
        x = jnp.concatenate([before, x, after], axis=dim)
    return x


def rows_first(field):
    return (
        field[..., :-4, :]
        - 8.0 * field[..., 1:-3, :]
        + 8.0 * field[..., 3:-1, :]
        - field[..., 4:, :]
    ) / 12.0


def cols_first(field):
    return (
        field[..., :-4] - 8.0 * field[..., 1:-3] + 8.0 * field[..., 3:-1] - field[..., 4:]
    ) / 12.0


def rows_second(field):
    return (
        -field[..., :-4, :]
        + 16.0 * field[..., 1:-3, :]
        - 30.0 * field[..., 2:-2, :]
        + 16.0 * field[..., 3:-1, :]
        - field[..., 4:, :]
    ) / 12.0


def second_column_split(field):
    return (
        -field[..., :-4]
        + 16.0 * field[..., 1:-3]
        - 30.0 * field[..., 2:-2]
        + 16.0 * field[..., 3:-1]
        - field[..., 4:]
    ) / 12.0


def surface(grad_a, grad_b, curve_aa, curve_bb, curve_ab):
    tan_a = (1.0 + grad_a[0], grad_a[1], grad_a[2])
    tan_b = (grad_b[0], 1.0 + grad_b[1], grad_b[2])
    normal = (
        tan_a[1] * tan_b[2] - tan_a[2] * tan_b[1],
        tan_a[2] * tan_b[0] - tan_a[0] * tan_b[2],
        tan_a[0] * tan_b[1] - tan_a[1] * tan_b[0],
    )
    area_stretch_factor = jnp.sqrt(
        normal[0] * normal[0] + normal[1] * normal[1] + normal[2] * normal[2]
    )
    unit = (
        normal[0] / area_stretch_factor,
        normal[1] / area_stretch_factor,
        normal[2] / area_stretch_factor,
    )
    first_edge_term = tan_a[0] * tan_a[0] + tan_a[1] * tan_a[1] + tan_a[2] * tan_a[2]
    first_f = tan_a[0] * tan_b[0] + tan_a[1] * tan_b[1] + tan_a[2] * tan_b[2]
    first_g = tan_b[0] * tan_b[0] + tan_b[1] * tan_b[1] + tan_b[2] * tan_b[2]
    second_l = curve_aa[0] * unit[0] + curve_aa[1] * unit[1] + curve_aa[2] * unit[2]
    second_m = curve_ab[0] * unit[0] + curve_ab[1] * unit[1] + curve_ab[2] * unit[2]
    second_n = curve_bb[0] * unit[0] + curve_bb[1] * unit[1] + curve_bb[2] * unit[2]
    curvature = (first_edge_term * second_n - 2.0 * first_f * second_m + first_g * second_l) / (
        2.0 * area_stretch_factor * area_stretch_factor
    )
    omega = (grad_a[3] / area_stretch_factor, grad_b[3] / area_stretch_factor)
    return (unit, curvature, omega)


def factors(length):
    inner = min(length, 256)
    return (length // inner, inner)


def angles(count_one, count_two, modulus):
    sample_lattice = (
        jnp.arange(count_one, dtype=jnp.int32)[:, None]
        * jnp.arange(count_two, dtype=jnp.int32)[None, :]
        % modulus
    )
    theta = sample_lattice.astype(jnp.float32) * (2.0 * math.pi / modulus)
    return (jnp.cos(theta), jnp.sin(theta))


def rotation(cos_table, sin_table, sense):
    top = jnp.stack([cos_table, sense * sin_table])
    low = jnp.stack([-sense * sin_table, cos_table])
    return jnp.stack([top, low])


def twisted(sheet_portion, cos_table, sin_table, sense):
    twist_re = sheet_portion[0] * cos_table + sense * sheet_portion[1] * sin_table
    twist_im = sheet_portion[1] * cos_table - sense * sheet_portion[0] * sin_table
    return jnp.stack([twist_re, twist_im])


def forward(values, length, kept, real_input):
    outer, inner = factors(length)
    cos_outer, sin_outer = angles(outer, outer, outer)
    if real_input:
        leading = values.shape[:-1]
        sample_lattice = values.reshape(leading + (outer, inner))
        lookup_array = jnp.stack([cos_outer, -sin_outer])
        sheet_portion = jnp.einsum(
            "...lm,zln->z...nm", sample_lattice, lookup_array, precision=largest_wavenumber
        )
    else:
        leading = values.shape[1:-1]
        sample_lattice = values.reshape((2,) + leading + (outer, inner))
        sheet_portion = jnp.einsum(
            "s...ab,tsac->t...cb",
            sample_lattice,
            rotation(cos_outer, sin_outer, 1.0),
            precision=largest_wavenumber,
        )
    cos_twist, sin_twist = angles(outer, inner, length)
    sheet_portion = twisted(sheet_portion, cos_twist, sin_twist, 1.0)
    cos_inner, sin_inner = angles(inner, kept, inner)
    result = jnp.einsum(
        "s...cb,tsbd->t...cd",
        sheet_portion,
        rotation(cos_inner, sin_inner, 1.0),
        precision=largest_wavenumber,
    )
    return result.reshape((2,) + leading + (outer * kept,))


def inverse(values, length, kept, want_imag):
    outer, inner = factors(length)
    leading = values.shape[1:-1]
    sample_lattice = values.reshape((2,) + leading + (outer, kept))
    cos_inner, sin_inner = angles(kept, inner, inner)
    sheet_portion = jnp.einsum(
        "s...cd,tsdb->t...cb",
        sample_lattice,
        rotation(cos_inner, sin_inner, -1.0),
        precision=largest_wavenumber,
    )
    cos_twist, sin_twist = angles(outer, inner, length)
    sheet_portion = twisted(sheet_portion, cos_twist, sin_twist, -1.0)
    cos_outer, sin_outer = angles(outer, outer, outer)
    if want_imag:
        result = jnp.einsum(
            "s...cb,tsca->t...ab",
            sheet_portion,
            rotation(cos_outer, sin_outer, -1.0),
            precision=largest_wavenumber,
        )
        return result.reshape((2,) + leading + (length,)) / length
    lookup_array = jnp.stack([cos_outer, -sin_outer])
    result = jnp.einsum(
        "s...cb,sca->...ab", sheet_portion, lookup_array, precision=largest_wavenumber
    )
    return result.reshape(leading + (length,)) / length


def wavenumbers(length, kept, positions):
    outer, inner = factors(length)
    number = positions // kept + outer * (positions % kept)
    signed = jnp.where(number >= length // 2, number - length, number)
    return (signed.astype(jnp.float32) / length, number == length // 2)


def local(shift_plane, height, dipole):
    fields = jnp.concatenate([shift_plane, height[None], dipole[None]], 0)
    padded = padded_2(fields, (("tr", 1), ("tc", 2)), 2)
    grad_a = rows_first(padded)[..., 2:-2]
    grad_b = cols_first(padded)[..., 2:-2, :]
    curve_aa = rows_second(padded[:3])[..., 2:-2]
    curve_bb = second_column_split(padded[:3])[..., 2:-2, :]
    curve_ab = rows_first(cols_first(padded[:3]))
    unit, curvature, omega = surface(grad_a, grad_b, curve_aa, curve_bb, curve_ab)
    vorticity = jnp.stack([omega[0], omega[1]])
    sheet_rows = lax.all_to_all(vorticity, "tc", split_axis=1, concat_axis=2, tiled=True)
    col_count = sheet_rows.shape[-1]
    row_count = height.shape[0] * lax.axis_size("tr")
    col_outer, col_inner = factors(col_count)
    row_outer, row_inner = factors(row_count)
    kept = col_inner // 2
    row_spec = forward(sheet_rows, col_count, kept, True)
    stacked = row_spec.reshape((4,) + row_spec.shape[2:])
    columns = lax.all_to_all(stacked, ("tr", "tc"), split_axis=2, concat_axis=1, tiled=True)
    columns = jnp.swapaxes(columns, 1, 2)
    local_width = columns.shape[1]
    full = forward(columns.reshape((2, 2) + columns.shape[1:]), row_count, row_inner, False)
    complete_real_part = full[0]
    full_im = full[1]
    place = lax.axis_index(("tr", "tc")) * local_width + jnp.arange(local_width, dtype=jnp.int32)
    freq_two, nyquist_two = wavenumbers(col_count, kept, place)
    freq_one, nyquist_one = wavenumbers(
        row_count, row_inner, jnp.arange(row_count, dtype=jnp.int32)
    )
    freq_one = freq_one[None, :]
    freq_two = freq_two[:, None]
    radius = jnp.sqrt(freq_one * freq_one + freq_two * freq_two)
    live = (
        jnp.logical_not(nyquist_one[None, :])
        & jnp.logical_not(nyquist_two[:, None])
        & (radius > 0.0)
    )
    factor = jnp.where(live, 0.5 / jnp.where(live, radius, 1.0), 0.0)
    summed_re = factor * (freq_one * complete_real_part[0] + freq_two * complete_real_part[1])
    summed_im = factor * (freq_one * full_im[0] + freq_two * full_im[1])
    speed_parts = inverse(jnp.stack([summed_im, -summed_re]), row_count, row_inner, True)
    partial_value = jnp.swapaxes(speed_parts, 1, 2)
    back_rows = lax.all_to_all(partial_value, ("tr", "tc"), split_axis=1, concat_axis=2, tiled=True)
    weights = (
        jnp.full((col_outer, kept), 2.0, jnp.float32).at[0, 0].set(1.0).reshape(col_outer * kept)
    )
    speed_rows = inverse(back_rows * weights, col_count, kept, False)
    speed = lax.all_to_all(speed_rows, "tc", split_axis=1, concat_axis=0, tiled=True)
    velocity_update = jnp.stack([speed * unit[0], speed * unit[1], speed * unit[2]])
    dipole_update = -2.0 * 0.5 * 0.5 * height + 0.3 * curvature + 0.5 * speed * speed
    return (velocity_update, dipole_update)


def solution(mesh):
    in_specs = (
        P(None, ("groups", "tr"), "tc"),
        P(("groups", "tr"), "tc"),
        P(("groups", "tr"), "tc"),
    )
    out_specs = (P(None, ("groups", "tr"), "tc"), P(("groups", "tr"), "tc"))
    return jax.shard_map(local, mesh=mesh, in_specs=in_specs, out_specs=out_specs, check_vma=False)
```

profile of v0, /device:TPU:21, one launch (start us, length us, event | category | flops | bytes accessed | tf_op | source)
XLA Modules:
  0.0 736.3 jit_solution(17802370308646644525)
XLA Ops:
  5.6 1.7 collective-permute-done
  7.4 8.5 %pad_maximum_fusion.1 = f32[4,516,2048]{2,1,0:T(8,128)S(1)} fusion(f32[4,2,2048]{2,1,0:T(2,128)S(1)} %copy.106, f32[1,512,2048]{2,1,0:T(8,128)S(1)} %bitcast.310, f32[1,512,2048]{2,1,0:T(8,128)S(1)} %bitcast.306, f32[2,512,2048]{2,1,0:T(8,128)S(1)} %bitcast.303, f32[4,2,2048]{2,1,0:T(2,128)S(1)} %copy.105), kind=kLoop, calls=%fused_computation.14 | loop fusion | flops 16908288 | bytes 33816576 | tf_op jit(solution)/shard_map/concatenate | solution.py:20
  15.9 5.8 copy-done
  22.9 2.1 collective-permute-start.2
  27.0 22.0 %concatenate.26 = f32[4,516,2052]{2,1,0:T(8,128)} concatenate(f32[4,516,2]{2,1,0:T(8,128)S(1)} %copy.109, f32[4,516,2048]{2,1,0:T(8,128)} %copy-done, f32[4,516,2]{2,1,0:T(8,128)S(1)} %copy.110), dimensions={2} | concatenate | bytes 33882624 | tf_op jit(solution)/shard_map/concatenate | solution.py:20
  49.0 31.9 %maximum_maximum_fusion = (f32[4,516,2050]{2,1,0:T(8,128)}, f32[4,516,2050]{2,1,0:T(8,128)}) fusion(f32[4,2,2048]{2,1,0:T(2,128)S(1)} %copy.106, f32[1,512,2048]{2,1,0:T(8,128)} %bitcast.309, f32[1,512,2048]{2,1,0:T(8,128)} %bitcast.305, f32[2,512,2048]{2,1,0:T(8,128)} %param.5, f32[4,2,2048]{2,1,0:T(2,128)S(1)} %copy.105, f32[4,516,2]{2,1,0:T(8,128)S(1)} %copy.109, ...), kind=kLoop, calls=%fused_computation | loop fusion | flops 42312000 | bytes 50790912 | tf_op jit(solution)/shard_map/concatenate | solution.py:20
  80.9 31.6 %fusion = f32[4,512,2052]{2,1,0:T(8,128)} fusion(f32[4,516,2052]{2,1,0:T(8,128)} %concatenate.26), kind=kLoop, calls=%fused_computation.3 | loop fusion | flops 25214976 | bytes 84049920 | tf_op jit(solution)/shard_map/div | solution.py:25
  112.6 34.9 %fusion.3 = f32[4,516,2048]{2,1,0:T(8,128)} fusion(f32[4,516,2050]{2,1,0:T(8,128)} %get-tuple-element.26, f32[4,516,2050]{2,1,0:T(8,128)} %get-tuple-element.25), kind=kLoop, calls=%fused_computation.9 | loop fusion | flops 25362432 | bytes 84541440 | tf_op jit(solution)/shard_map/div | solution.py:34
  147.5 18.2 %slice_multiply_fusion.11 = (f32[1,512,2048]{2,1,0:T(8,128)}, f32[1,512,2048]{2,1,0:T(8,128)S(1)}, f32[1,512,2048]{2,1,0:T(8,128)}, f32[1,512,2048]{2,1,0:T(8,128)}, f32[1,512,2048]{2,1,0:T(8,128)}) fusion(f32[4,512,2052]{2,1,0:T(8,128)} %fusion, f32[4,516,2048]{2,1,0:T(8,128)} %fusion.3), kind=kLoop, calls=%fused_computation.92 | loop fusion | flops 17825792 | bytes 50331648 | tf_op jit(solution)/shard_map/div | solution.py:84
  165.7 4.7 slice_multiply_fusion.10
  171.8 7.3 copy.113
  179.1 10.7 %all_to_all.64 = f32[2,512,2048]{2,0,1:T(2,128)S(1)} all-to-all(f32[2,512,2048]{2,0,1:T(2,128)S(1)} %copy.113), channel_id=1, replica_groups=mesh['groups'=2,'tr'=8,'tc'=2] {'tc'}, dimensions={1} | all-to-all | bytes 16777216 | tf_op jit(solution)/shard_map/all_to_all | solution.py:192
  189.7 9.7 %copy.170 = f32[2,2,256,2048]{3,1,2,0:T(2,128)} copy(f32[2,2,256,2048]{3,0,2,1:T(2,128)S(1)} %bitcast.312) | data formatting | bytes 16777216 | tf_op jit(solution)/shard_map/all_to_all | solution.py:192
  199.5 11.5 %reshape.791 = f32[2,256,16,256,1]{3,2,1,0,4:T(8,128)} reshape(f32[2,256,2,2048]{3,2,1,0:T(2,128)} %bitcast.313) | data formatting | bytes 16777216 | tf_op jit(solution)/shard_map/reshape | solution.py:120
  211.0 16.0 %convolution_bitcast_fusion = f32[2,2,256,16,256]{4,3,2,1,0:T(8,128)S(1)} fusion(f32[2,256,16,256,1]{3,2,1,0,4:T(8,128)} %reshape.791, f32[1,16,16]{1,2,0:T(8,128)S(1)} %get-tuple-element.58, f32[1,16,16]{1,2,0:T(8,128)S(1)} %get-tuple-element.59), kind=kOutput, calls=%fused_computation.53 | convolution fusion | flops 805306880 | bytes 25167872 | tf_op jit(solution)/shard_map/...lm,zln->z...nm/dot_general | solution.py:122
  227.0 7.1 multiply_add_fusion
  234.1 6.9 pad_maximum_fusion.2
  241.0 23.2 %fusion.6 = f32[2,128,2,256,16,1]{3,1,5,4,2,0:T(8,128)} fusion(f32[2,2,256,16,256]{4,3,2,1,0:T(8,128)S(1)} %pad_maximum_fusion.2, f32[1,2,256,128]{2,3,1,0:T(8,128)S(1)} %copy-done.12, f32[1,2,256,128]{2,3,1,0:T(8,128)S(1)} %copy-done.11), kind=kOutput, calls=%fused_computation.16 | convolution fusion | flops 12885032960 | bytes 25690112 | tf_op jit(solution)/shard_map/s...cb,tsbd->t...cd/dot_general | solution.py:137
  264.2 11.8 %copy.116 = f32[4,256,2048]{1,0,2:T(4,128)} copy(f32[4,256,2048]{1,2,0:T(8,128)} %bitcast.307) | data formatting | bytes 16777216 | tf_op jit(solution)/shard_map/reshape;reshape | solution.py:199
  276.0 10.2 %all-to-all-start.1 = ((f32[4,256,2048]{1,0,2:T(4,128)}), f32[4,256,2048]{1,0,2:T(4,128)}, u32[]{:S(2)}, u32[]{:S(2)}) async-start(f32[4,256,2048]{1,0,2:T(4,128)} %copy.116), calls=%async_computation.1 | async-start | bytes 16777216 | tf_op jit(solution)/shard_map/all_to_all | solution.py:200
  288.7 179.1 %all-to-all-done.1 = f32[4,256,2048]{1,0,2:T(4,128)} async-done(((f32[4,256,2048]{1,0,2:T(4,128)}), f32[4,256,2048]{1,0,2:T(4,128)}, u32[]{:S(2)}, u32[]{:S(2)}) %all-to-all-start.1) | async-done | bytes 8388640 | tf_op jit(solution)/shard_map/all_to_all | solution.py:200
  467.8 5.0 copy.117
  472.8 12.8 %fusion.69 = f32[2,2,128,16,256]{4,3,2,1,0:T(8,128)S(1)} fusion(f32[2,2,128,16,256]{4,2,3,1,0:T(8,128)S(1)} %bitcast.311, f32[1,2,16,16]{2,3,1,0:T(8,128)S(1)} %get-tuple-element.53, f32[1,2,16,16]{2,3,1,0:T(8,128)S(1)} %get-tuple-element.56), kind=kOutput, calls=%fused_computation.127 | convolution fusion | flops 805307392 | bytes 16781312 | tf_op jit(solution)/shard_map/s...ab,tsac->t...cb/dot_general | solution.py:128
  485.6 1.8 multiply_add_fusion.2
  488.4 18.4 %fusion.66 = f32[2,2,128,16,256]{2,4,3,1,0:T(8,128)S(1)} fusion(f32[2,2,128,16,256]{4,3,2,1,0:T(8,128)S(1)} %pad_maximum_fusion.5, f32[1,2,256,256]{2,3,1,0:T(8,128)S(1)} %get-tuple-element.43, f32[1,2,256,256]{2,3,1,0:T(8,128)S(1)} %get-tuple-element.46), kind=kOutput, calls=%fused_computation.126 | convolution fusion | flops 12885164032 | bytes 17825792 | tf_op jit(solution)/shard_map/s...cb,tsbd->t...cd/dot_general | solution.py:137
  506.8 2.9 fusion.82
  509.7 7.2 fusion.74
  516.9 1.4 multiply_add_fusion.3
  518.3 2.3 pad_maximum_fusion.7
  520.6 5.4 copy.122
  526.0 7.9 %fusion.59 = f32[2,128,16,256]{3,2,1,0:T(8,128)} fusion(f32[2,128,16,256]{3,2,0,1:T(8,128)} %copy.122, f32[1,2,16,16]{2,3,1,0:T(8,128)S(1)} %get-tuple-element.57, f32[1,2,16,16]{2,3,1,0:T(8,128)S(1)} %get-tuple-element.52), kind=kOutput, calls=%fused_computation.112 | convolution fusion | flops 403702784 | bytes 8392704 | tf_op jit(solution)/shard_map/s...cb,tsca->t...ab/dot_general | solution.py:161
  533.9 5.2 copy.146
  539.2 5.5 all-to-all-start.2
  545.7 34.2 %fusion.16 = (f32[3,516,2048]{2,1,0:T(8,128)}, f32[3,516,2048]{2,1,0:T(8,128)}) fusion(f32[4,516,2048]{2,1,0:T(8,128)} %copy-done, f32[4,516,2050]{2,1,0:T(8,128)} %get-tuple-element.26, f32[4,516,2050]{2,1,0:T(8,128)} %get-tuple-element.25), kind=kLoop, calls=%fused_computation.32 | loop fusion | flops 47554560 | bytes 88768512 | tf_op jit(solution)/shard_map/div | solution.py:50
  579.8 27.0 %fusion.17 = f32[3,512,2048]{2,1,0:T(8,128)} fusion(f32[3,516,2048]{2,1,0:T(8,128)} %get-tuple-element.22), kind=kLoop, calls=%fused_computation.35 | loop fusion | flops 18874368 | bytes 62914560 | tf_op jit(solution)/shard_map/div | solution.py:25
  606.8 28.6 %fusion.9 = f32[3,512,2052]{2,1,0:T(8,128)} fusion(f32[4,516,2052]{2,1,0:T(8,128)} %concatenate.26), kind=kLoop, calls=%fused_computation.20 | loop fusion | flops 28366848 | bytes 75644928 | tf_op jit(solution)/shard_map/div | solution.py:40
  636.6 2.5 copy.124
  639.0 6.8 fusion.63
  645.8 1.4 multiply_add_fusion.1
  647.3 4.0 pad_maximum_fusion.6
  651.3 10.3 %copy.126 = f32[2,256,16,256]{3,2,0,1:T(8,128)} copy(f32[2,256,16,256]{1,3,2,0:T(8,128)} %pad_maximum_fusion.6) | data formatting | bytes 16777216 | tf_op jit(solution)/shard_map/stack | solution.py:112
  661.6 7.7 %fusion.56 = f32[256,16,256]{2,1,0:T(8,128)} fusion(f32[2,256,16,256]{3,2,0,1:T(8,128)} %copy.126, f32[1,16,16]{1,2,0:T(8,128)S(1)} %get-tuple-element.58, f32[1,16,16]{1,2,0:T(8,128)S(1)} %copy-done.14), kind=kOutput, calls=%fused_computation.108 | convolution fusion | flops 403702272 | bytes 12584960 | tf_op jit(solution)/shard_map/s...cb,sca->...ab/dot_general | solution.py:169
  669.3 6.1 div.165
  675.4 4.8 copy.127
  680.2 8.1 %all_to_all.65 = f32[256,2,2048]{2,0,1:T(8,128)S(1)} all-to-all(f32[256,2,2048]{2,0,1:T(8,128)S(1)} %copy.127), channel_id=1, replica_groups=mesh['groups'=2,'tr'=8,'tc'=2] {'tc'}, dimensions={1} | all-to-all | bytes 8388608 | tf_op jit(solution)/shard_map/all_to_all | solution.py:229
  688.4 5.9 bitcast_multiply_fusion.5
  694.2 11.8 %pad_maximum_fusion.3 = f32[3,512,2048]{2,1,0:T(8,128)} fusion(f32[1,512,2048]{2,1,0:T(8,128)} %get-tuple-element.39, f32[1,512,2048]{2,1,0:T(8,128)} %get-tuple-element.38, f32[1,512,2048]{2,1,0:T(8,128)} %get-tuple-element.37), kind=kLoop, calls=%fused_computation.40 | loop fusion | flops 6291456 | bytes 25165824 | tf_op jit(solution)/shard_map/stack | solution.py:230
  706.0 29.8 %fusion.29 = f32[512,2048]{1,0:T(8,128)} fusion(f32[3,512,2052]{2,1,0:T(8,128)} %fusion.9, f32[3,512,2048]{2,1,0:T(8,128)} %fusion.17, f32[3,516,2048]{2,1,0:T(8,128)} %get-tuple-element.21, f32[256,2,2048]{2,0,1:T(8,128)} %copy-done.9, f32[1,512,2048]{2,1,0:T(8,128)} %get-tuple-element.20, f32[1,512,2048]{2,1,0:T(8,128)} %get-tuple-element.19, ...), kind=kLoop, calls=%fused_computation.59 | loop fusion | flops 57671680 | bytes 88080384 | tf_op jit(solution)/shard_map/add | solution.py:231
  (73 shorter events, 15.0 us)
Async XLA Ops:
  0.6 6.7 slice-start
  0.6 6.7 slice-start.1
  0.7 6.7 copy-start.1
  0.7 6.7 copy-start.5
  2.0 3.5 collective-permute-start.1
  3.2 4.1 collective-permute-start
  15.9 5.8 copy-start
  22.9 3.7 collective-permute-start.2
  25.0 1.2 collective-permute-start.3
  25.1 185.9 %copy-start.13 = (f32[1,16,16]{1,2,0:T(8,128)}, f32[1,16,16]{1,2,0:T(8,128)S(1)}, u32[]{:S(2)}) copy-start(f32[1,16,16]{1,2,0:T(8,128)S(1)} %get-tuple-element.59) | copy-start | bytes 3076
  165.7 4.7 copy-start.3
  165.7 5.0 copy-start.10
  234.1 6.9 copy-start.11
  234.1 6.9 copy-start.12
  276.0 191.8 %all-to-all-start.1 = ((f32[4,256,2048]{1,0,2:T(4,128)}), f32[4,256,2048]{1,0,2:T(4,128)}, u32[]{:S(2)}, u32[]{:S(2)}) async-start(f32[4,256,2048]{1,0,2:T(4,128)} %copy.116), calls=%async_computation.1 | async-start | bytes 16777216 | tf_op jit(solution)/shard_map/all_to_all | solution.py:200
  539.2 97.4 %all-to-all-start.2 = ((f32[2,4096,128]{2,0,1:T(2,128)}), f32[2,4096,128]{2,0,1:T(2,128)}, u32[]{:S(2)}, u32[]{:S(2)}) async-start(f32[2,4096,128]{2,0,1:T(2,128)} %bitcast.314), calls=%async_computation.2 | async-start | bytes 8388608 | tf_op jit(solution)/shard_map/all_to_all | solution.py:224
  635.4 3.6 copy-start.15
  651.3 10.3 %copy-start.14 = (f32[1,16,16]{1,2,0:T(8,128)S(1)}, f32[1,16,16]{1,2,0:T(8,128)}, u32[]{:S(2)}) copy-start(f32[1,16,16]{1,2,0:T(8,128)} %copy-done.13) | copy-start | bytes 3076
  675.4 12.9 %copy-start.7 = (f32[1,512,2048]{2,1,0:T(8,128)S(1)}, f32[1,512,2048]{2,1,0:T(8,128)}, u32[]{:S(2)}) copy-start(f32[1,512,2048]{2,1,0:T(8,128)} %get-tuple-element.19) | copy-start | bytes 12582916
  675.4 12.9 %copy-start.8 = (f32[1,512,2048]{2,1,0:T(8,128)S(1)}, f32[1,512,2048]{2,1,0:T(8,128)}, u32[]{:S(2)}) copy-start(f32[1,512,2048]{2,1,0:T(8,128)} %get-tuple-element.20) | copy-start | bytes 12582916
  680.2 8.1 %copy-start.4 = (f32[1,512,2048]{2,1,0:T(8,128)S(1)}, f32[1,512,2048]{2,1,0:T(8,128)}, u32[]{:S(2)}) copy-start(f32[1,512,2048]{2,1,0:T(8,128)} %copy-done.3) | copy-start | bytes 12582916
  680.2 8.1 %copy-start.6 = (f32[1,512,2048]{2,1,0:T(8,128)S(1)}, f32[1,512,2048]{2,1,0:T(8,128)}, u32[]{:S(2)}) copy-start(f32[1,512,2048]{2,1,0:T(8,128)} %get-tuple-element.18) | copy-start | bytes 12582916
  688.3 5.9 copy-start.9
  694.2 11.8 %copy-start.2 = (f32[512,2048]{1,0:T(8,128)S(1)}, f32[512,2048]{1,0:T(8,128)}, u32[]{:S(2)}) copy-start(f32[512,2048]{1,0:T(8,128)} %param.6) | copy-start | bytes 12582916
where the time goes:
time: 746 us; the launch traced here: 736 us
  other arithmetic  304 us (41%)
  waiting for transfers between devices  183 us (25%)
  local copies, waits for them, and re-layouts  110 us (15%)
  matrix products  100 us (13%)
  starting transfers between devices  19.4 us (3%)
  blocking collectives  18.8 us (3%)
    all_to_all x1, waiting for transfers between devices, local(): lax.all_to_all(stacked, ('tr', 'tc'), split_axis=2, concat_axis=1, tiled=...  179 us
    div x2, other arithmetic, rows_first(): (field[..., :-4, :] - 8.0 * field[..., 1:-3, :] + 8.0 * field[..., 3:-1,...  58.6 us
    dot_general x2, matrix products, forward(): jnp.einsum('s...cb,tsbd->t...cd', sheet_portion, rotation(cos_inner, sin_...  41.6 us
    concatenate x2, other arithmetic, padded_2(): x = jnp.concatenate([before, x, after], axis=dim)  40.4 us
    div x1, other arithmetic, cols_first(): (field[..., :-4] - 8.0 * field[..., 1:-3] + 8.0 * field[..., 3:-1] - fiel...  34.9 us
    div x1, other arithmetic, second_column_split(): (-field[..., :-4] + 16.0 * field[..., 1:-3] - 30.0 * field[..., 2:-2] + 1...  34.2 us
    add x1, other arithmetic, local(): -2.0 * 0.5 * 0.5 * height + 0.3 * curvature + 0.5 * speed * speed  29.8 us
    div x1, other arithmetic, rows_second(): (-field[..., :-4, :] + 16.0 * field[..., 1:-3, :] - 30.0 * field[..., 2:-...  28.6 us
  transfers between devices with their start and end apart: 6, of which 4 were waited for; matrix products, arithmetic and copies ran while one was open for 13% of the time, Pallas kernels for 0%

commit v1 on v0

--- a/solution.py
+++ b/solution.py
@@ -2,7 +2,10 @@
 
 import jax
 import jax.numpy as jnp
+import numpy as np
 from jax import lax
+from jax.experimental import pallas as pl
+from jax.experimental.pallas import tpu as pltpu
 from jax.sharding import PartitionSpec as P
 
 largest_wavenumber = lax.Precision.HIGHEST
@@ -232,6 +235,490 @@
     return (velocity_update, dipole_update)
 
 
+LANES = 128
+SUB = 8
+VMEM_BYTES = 58 * 1024 * 1024
+
+
+def params():
+    return pltpu.CompilerParams(vmem_limit_bytes=VMEM_BYTES)
+
+
+def two_halves(table):
+    table = np.asarray(table, np.float32)
+    high = table.astype(jnp.bfloat16)
+    low = (table - high.astype(np.float32)).astype(jnp.bfloat16)
+    return np.stack([high, low])
+
+
+def unit_circle(count_one, count_two, modulus):
+    theta = np.arange(count_one)[:, None] * np.arange(count_two)[None, :] % modulus
+    theta = theta * (2.0 * math.pi / modulus)
+    return np.cos(theta), np.sin(theta)
+
+
+def split(x):
+    high = x.astype(jnp.bfloat16)
+    low = (x - high.astype(jnp.float32)).astype(jnp.bfloat16)
+    return high, low
+
+
+def product(a, b):
+    dot = lambda p, q: jnp.dot(p, q, preferred_element_type=jnp.float32)
+    return dot(a[0], b[0]) + (dot(a[0], b[1]) + dot(a[1], b[0]))
+
+
+def plus(p, q):
+    return q if p is None else p if q is None else p + q
+
+
+def minus(p, q):
+    if q is None:
+        return p
+    return -q if p is None else p - q
+
+
+def turned(z, number, size, sense):
+    re, im = z
+    number = number % size
+    if number == 0:
+        return z
+    if 4 * number == size:
+        if sense > 0:
+            return (im, None if re is None else -re)
+        return (None if im is None else -im, re)
+    c = math.cos(2.0 * math.pi * number / size)
+    s = -sense * math.sin(2.0 * math.pi * number / size)
+    if 8 * number == size:
+        r = math.sqrt(0.5)
+        if im is None:
+            return (re * r, re * (-sense * r))
+        if sense > 0:
+            return ((re + im) * r, (im - re) * r)
+        return ((re - im) * r, (im + re) * r)
+    if im is None:
+        return (re * c, re * s)
+    return (re * c - im * s, re * s + im * c)
+
+
+def butterflies(z, sense):
+    size = len(z)
+    if size == 1:
+        return z
+    even = butterflies(z[0::2], sense)
+    odd = butterflies(z[1::2], sense)
+    odd = [turned(o, k, size, sense) for k, o in enumerate(odd)]
+    head = [(plus(e[0], o[0]), plus(e[1], o[1])) for e, o in zip(even, odd)]
+    tail = [(minus(e[0], o[0]), minus(e[1], o[1])) for e, o in zip(even, odd)]
+    return head + tail
+
+
+def twist(z, c, s, sense):
+    re, im = z
+    if im is None:
+        return (re * c, re * s * (-sense))
+    if sense > 0:
+        return (re * c + im * s, im * c - re * s)
+    return (re * c - im * s, im * c + re * s)
+
+
+def stencil(shift_plane, height, dipole, halos, tc, want_omega):
+    rows, cols = height.shape
+    block = min(64, rows // tc)
+    steps = rows // block
+    chunk = min(256, cols)
+    wide = min(1024, cols)
+    groups = block // SUB
+    count = 4 if want_omega else 3
+    tall = block + 2 * SUB
+    last = rows // SUB - 1
+
+    def kernel(*refs):
+        if want_omega:
+            arrays, refs = (refs[:9], refs[9:])
+            top, bottom, left, right, omega_ref, pad, slope = refs
+        else:
+            arrays, refs = (refs[:6], refs[6:])
+            top, bottom, left, right, unit_ref, base_ref, pad, slope, bend = refs
+        i = pl.program_id(0)
+        for f in range(count):
+            trio = arrays[:3] if f < 2 else arrays[3 * (f - 1) : 3 * f]
+            take = (lambda r: r[f]) if f < 2 else (lambda r: r[...])
+            cur, prev, nxt = trio
+            pad[f, SUB : SUB + block, LANES : LANES + cols] = take(cur)
+            pad[f, 0:SUB, LANES : LANES + cols] = jnp.where(i == 0, top[f], take(prev))
+            pad[f, SUB + block :, LANES : LANES + cols] = jnp.where(
+                i == steps - 1, bottom[f], take(nxt)
+            )
+            pad[f, :, 0:LANES] = left[f, pl.ds(pl.multiple_of(i * block, SUB), tall), :]
+            pad[f, :, LANES + cols :] = right[f, pl.ds(pl.multiple_of(i * block, SUB), tall), :]
+
+        def along(g, carry):
+            r = pl.ds(pl.multiple_of(g * SUB, SUB), SUB)
+            for f in range(count):
+                for j in range(cols // wide):
+                    width = wide + 2 * LANES
+                    x = pad[f, r, j * wide : j * wide + width]
+                    roll = lambda k: pltpu.roll(x, k % width, 1)[:, LANES : LANES + wide]
+                    m2, m1, p1, p2 = roll(2), roll(1), roll(-1), roll(-2)
+                    here = slice(j * wide, (j + 1) * wide)
+                    slope[f, r, here] = ((m2 - p2) + 8.0 * (p1 - m1)) * (1.0 / 12.0)
+                    if not want_omega:
+                        mid = x[:, LANES : LANES + wide]
+                        bend[f, r, here] = (16.0 * (m1 + p1) - (m2 + p2) - 30.0 * mid) * (
+                            1.0 / 12.0
+                        )
+            return carry
+
+        lax.fori_loop(0, tall // SUB, along, 0)
+
+        def across(j, carry):
+            inner = pl.ds(pl.multiple_of(j * chunk, LANES), chunk)
+            outer = pl.ds(pl.multiple_of(j * chunk + LANES, LANES), chunk)
+            for g in range(groups):
+                at = lambda ref, f, k, lanes: ref[f, SUB * (g + 1) + k : SUB * (g + 2) + k, lanes]
+
+                def first(ref, f, lanes):
+                    return (
+                        (at(ref, f, -2, lanes) - at(ref, f, 2, lanes))
+                        + 8.0 * (at(ref, f, 1, lanes) - at(ref, f, -1, lanes))
+                    ) * (1.0 / 12.0)
+
+                ga = [first(pad, f, outer) for f in range(count)]
+                gb = [at(slope, f, 0, inner) for f in range(count)]
+                ta = (1.0 + ga[0], ga[1], ga[2])
+                tb = (gb[0], 1.0 + gb[1], gb[2])
+                n = (
+                    ta[1] * tb[2] - ta[2] * tb[1],
+                    ta[2] * tb[0] - ta[0] * tb[2],
+                    ta[0] * tb[1] - ta[1] * tb[0],
+                )
+                inv = 1.0 / jnp.sqrt(n[0] * n[0] + n[1] * n[1] + n[2] * n[2])
+                out = slice(g * SUB, (g + 1) * SUB)
+                if want_omega:
+                    omega_ref[0, 0, out, inner] = ga[3] * inv
+                    omega_ref[0, 1, out, inner] = gb[3] * inv
+                    continue
+                unit = [v * inv for v in n]
+                for f in range(3):
+                    unit_ref[f, out, inner] = unit[f]
+                big_e = ta[0] * ta[0] + ta[1] * ta[1] + ta[2] * ta[2]
+                big_f = ta[0] * tb[0] + ta[1] * tb[1] + ta[2] * tb[2]
+                big_g = tb[0] * tb[0] + tb[1] * tb[1] + tb[2] * tb[2]
+                sl = sm = sn = None
+                for f in range(3):
+                    mid = at(pad, f, 0, outer)
+                    aa = (
+                        16.0 * (at(pad, f, -1, outer) + at(pad, f, 1, outer))
+                        - (at(pad, f, -2, outer) + at(pad, f, 2, outer))
+                        - 30.0 * mid
+                    ) * (1.0 / 12.0)
+                    sl = plus(sl, aa * unit[f])
+                    sm = plus(sm, first(slope, f, inner) * unit[f])
+                    sn = plus(sn, at(bend, f, 0, inner) * unit[f])
+                curvature = (big_e * sn - 2.0 * big_f * sm + big_g * sl) * (0.5 * inv * inv)
+                base_ref[out, inner] = -0.5 * at(pad, 2, 0, outer) + 0.3 * curvature
+            return carry
+
+        lax.fori_loop(0, cols // chunk, across, 0)
+
+    per = block // SUB
+    plane = [
+        pl.BlockSpec((block, cols), lambda i: (i, 0)),
+        pl.BlockSpec((SUB, cols), lambda i: (jnp.maximum(i * per - 1, 0), 0)),
+        pl.BlockSpec((SUB, cols), lambda i: (jnp.minimum((i + 1) * per, last), 0)),
+    ]
+    pair = [
+        pl.BlockSpec((2, block, cols), lambda i: (0, i, 0)),
+        pl.BlockSpec((2, SUB, cols), lambda i: (0, jnp.maximum(i * per - 1, 0), 0)),
+        pl.BlockSpec((2, SUB, cols), lambda i: (0, jnp.minimum((i + 1) * per, last), 0)),
+    ]
+    whole = [pl.BlockSpec(h.shape, lambda i: (0, 0, 0)) for h in halos]
+    ins = [shift_plane] * 3 + [height] * 3 + ([dipole] * 3 if want_omega else [])
+    scratch = [
+        pltpu.VMEM((count, tall, cols + 2 * LANES), jnp.float32),
+        pltpu.VMEM((count, tall, cols), jnp.float32),
+    ]
+    f32 = lambda *dims: jax.ShapeDtypeStruct(dims, jnp.float32)
+    if want_omega:
+        half = steps // tc
+        out_shape = f32(tc, 2, rows // tc, cols)
+        out_specs = pl.BlockSpec((1, 2, block, cols), lambda i: (i // half, 0, i % half, 0))
+    else:
+        out_shape = (f32(3, rows, cols), f32(rows, cols))
+        out_specs = (
+            pl.BlockSpec((3, block, cols), lambda i: (0, i, 0)),
+            pl.BlockSpec((block, cols), lambda i: (i, 0)),
+        )
+        scratch.append(pltpu.VMEM((count, tall, cols), jnp.float32))
+    return pl.pallas_call(
+        kernel,
+        grid=(steps,),
+        in_specs=pair + plane * (count - 2) + whole,
+        out_specs=out_specs,
+        out_shape=out_shape,
+        scratch_shapes=scratch,
+        compiler_params=params(),
+        name="omega" if want_omega else "geometry",
+    )(*ins, *halos)
+
+
+def row_tables(outer, inner, length):
+    c, s = unit_circle(outer, inner, length)
+    table = np.stack([c, s]).astype(np.float32)
+    return jnp.broadcast_to(jnp.asarray(table)[:, :, None, :], (2, outer, SUB, inner))
+
+
+def row_forward(omega, outer, inner):
+    tc, _, rows, cols = omega.shape
+    kept = inner // 2
+    length = tc * cols
+    block = min(64, rows)
+    per = outer // tc
+    c, s = unit_circle(inner, kept, inner)
+    matrix = two_halves(np.block([[c, -s], [s, c]]))
+
+    def kernel(x_ref, tw_ref, m_ref, out_ref, mid):
+        def step(g, carry):
+            r = pl.ds(pl.multiple_of(g * SUB, SUB), SUB)
+            for j in range(0, inner, LANES):
+                z = []
+                for l in range(outer):
+                    at = (l % per) * inner + j
+                    z.append((x_ref[l // per, 0, r, at : at + LANES], None))
+                z = butterflies(z, 1.0)
+                for n in range(outer):
+                    re, im = z[n]
+                    if n:
+                        re, im = twist(
+                            z[n],
+                            tw_ref[0, n, :, j : j + LANES],
+                            tw_ref[1, n, :, j : j + LANES],
+                            1.0,
+                        )
+                    if im is None:
+                        im = jnp.zeros_like(re)
+                    mid[n, r, j : j + LANES] = re
+                    mid[n, r, inner + j : inner + j + LANES] = im
+            return carry
+
+        lax.fori_loop(0, block // SUB, step, 0)
+
+        def finish(n, carry):
+            y = product(split(mid[n]), (m_ref[0], m_ref[1]))
+            out_ref[n, 0, 0] = y[:, :kept]
+            out_ref[n, 1, 0] = y[:, kept:]
+            return carry
+
+        lax.fori_loop(0, outer, finish, 0, unroll=4)
+
+    return pl.pallas_call(
+        kernel,
+        grid=(2, rows // block),
+        in_specs=[
+            pl.BlockSpec((tc, 1, block, cols), lambda p, i: (0, p, i, 0)),
+            pl.BlockSpec((2, outer, SUB, inner), lambda p, i: (0, 0, 0, 0)),
+            pl.BlockSpec(matrix.shape, lambda p, i: (0, 0, 0)),
+        ],
+        out_specs=pl.BlockSpec((outer, 2, 1, block, kept), lambda p, i: (0, 0, p, i, 0)),
+        out_shape=jax.ShapeDtypeStruct((outer, 2, 2, rows, kept), jnp.float32),
+        scratch_shapes=[pltpu.VMEM((outer, block, 2 * inner), jnp.float32)],
+        compiler_params=params(),
+        name="rows_forward",
+    )(omega, row_tables(outer, inner, length), jnp.asarray(matrix))
+
+
+def column_middle(spectra, freq_two, live_two, outer, inner):
+    length = outer * inner
+    width = spectra.shape[-1]
+    c, s = unit_circle(outer, inner, length)
+    table = jnp.asarray(np.stack([c, s]).astype(np.float32))
+    table = jnp.broadcast_to(table[..., None], (2, outer, inner, width))
+    c, s = unit_circle(inner, inner, inner)
+    matrix = two_halves(np.concatenate([c, s], 0))
+
+    def kernel(x_ref, tw_ref, m_ref, f_ref, live_ref, out_ref, mid):
+        def down(g, carry):
+            r = pl.ds(pl.multiple_of(g * SUB, SUB), SUB)
+            for p in range(2):
+                z = [(x_ref[a, 0, p, r, :], x_ref[a, 1, p, r, :]) for a in range(outer)]
+                z = butterflies(z, 1.0)
+                for k in range(outer):
+                    re, im = z[k] if k == 0 else twist(z[k], tw_ref[0, k, r], tw_ref[1, k, r], 1.0)
+                    mid[k, r, (2 * p) * width : (2 * p + 1) * width] = re
+                    mid[k, r, (2 * p + 1) * width : (2 * p + 2) * width] = im
+            return carry
+
+        lax.fori_loop(0, inner // SUB, down, 0)
+        fre_two = f_ref[...]
+        live_cols = live_ref[...]
+        weights = (m_ref[0], m_ref[1])
+
+        def turn(k, carry):
+            y = product(weights, split(mid[k]))
+            parts = []
+            for p in range(2):
+                lo = slice((2 * p) * width, (2 * p + 1) * width)
+                hi = slice((2 * p + 1) * width, (2 * p + 2) * width)
+                parts.append((y[:inner, lo] + y[inner:, hi], y[:inner, hi] - y[inner:, lo]))
+            number = k + outer * lax.broadcasted_iota(jnp.int32, (inner, width), 0)
+            signed = jnp.where(number >= length // 2, number - length, number)
+            fre_one = signed.astype(jnp.float32) * (1.0 / length)
+            radius = jnp.sqrt(fre_one * fre_one + fre_two * fre_two)
+            live = (number != length // 2) & (live_cols > 0.0) & (radius > 0.0)
+            factor = jnp.where(live, 0.5 / jnp.where(live, radius, 1.0), 0.0)
+            one = factor * fre_one
+            two = factor * fre_two
+            sum_re = one * parts[0][0] + two * parts[1][0]
+            sum_im = one * parts[0][1] + two * parts[1][1]
+            w = jnp.concatenate([sum_im, -sum_re], 1)
+            y = product(weights, split(w))
+            mid[k, :, :width] = y[:inner, :width] - y[inner:, width:]
+            mid[k, :, width : 2 * width] = y[:inner, width:] + y[inner:, :width]
+            return carry
+
+        lax.fori_loop(0, outer, turn, 0)
+
+        def up(g, carry):
+            r = pl.ds(pl.multiple_of(g * SUB, SUB), SUB)
+            z = []
+            for k in range(outer):
+                v = (mid[k, r, :width], mid[k, r, width : 2 * width])
+                z.append(v if k == 0 else twist(v, tw_ref[0, k, r], tw_ref[1, k, r], -1.0))
+            z = butterflies(z, -1.0)
+            for a in range(outer):
+                out_ref[a, 0, r, :] = z[a][0] * (1.0 / length)
+                out_ref[a, 1, r, :] = z[a][1] * (1.0 / length)
+            return carry
+
+        lax.fori_loop(0, inner // SUB, up, 0)
+
+    return pl.pallas_call(
+        kernel,
+        out_shape=jax.ShapeDtypeStruct((outer, 2, inner, width), jnp.float32),
+        scratch_shapes=[pltpu.VMEM((outer, inner, 4 * width), jnp.float32)],
+        compiler_params=params(),
+        name="columns",
+    )(spectra, table, jnp.asarray(matrix), freq_two, live_two)
+
+
+def row_inverse(partial, outer, inner, tc):
+    _, _, rows, kept = partial.shape
+    length = outer * inner
+    cols = length // tc
+    per = outer // tc
+    block = min(64, rows)
+    c, s = unit_circle(kept, inner, inner)
+    matrix = two_halves(np.block([[c, s], [-s, c]]) * (2.0 / length))
+
+    def kernel(x_ref, tw_ref, m_ref, out_ref, mid):
+        lane = lax.broadcasted_iota(jnp.int32, (block, kept), 1)
+
+        def start(n, carry):
+            weight = jnp.where((lane == 0) & (n == 0), 0.5, 1.0)
+            w = jnp.concatenate([x_ref[n, 0] * weight, x_ref[n, 1] * weight], 1)
+            mid[n] = product(split(w), (m_ref[0], m_ref[1]))
+            return carry
+
+        lax.fori_loop(0, outer, start, 0, unroll=4)
+
+        def step(g, carry):
+            r = pl.ds(pl.multiple_of(g * SUB, SUB), SUB)
+            for j in range(0, inner, LANES):
+                z = []
+                for n in range(outer):
+                    v = (mid[n, r, j : j + LANES], mid[n, r, inner + j : inner + j + LANES])
+                    if n:
+                        v = twist(
+                            v,
+                            tw_ref[0, n, :, j : j + LANES],
+                            tw_ref[1, n, :, j : j + LANES],
+                            -1.0,
+                        )
+                    z.append(v)
+                z = butterflies(z, -1.0)
+                for l in range(outer):
+                    at = (l % per) * inner + j
+                    out_ref[l // per, r, at : at + LANES] = z[l][0]
+            return carry
+
+        lax.fori_loop(0, block // SUB, step, 0)
+
+    return pl.pallas_call(
+        kernel,
+        grid=(rows // block,),
+        in_specs=[
+            pl.BlockSpec((outer, 2, block, kept), lambda i: (0, 0, i, 0)),
+            pl.BlockSpec((2, outer, SUB, inner), lambda i: (0, 0, 0, 0)),
+            pl.BlockSpec(matrix.shape, lambda i: (0, 0, 0)),
+        ],
+        out_specs=pl.BlockSpec((tc, block, cols), lambda i: (0, i, 0)),
+        out_shape=jax.ShapeDtypeStruct((tc, rows, cols), jnp.float32),
+        scratch_shapes=[pltpu.VMEM((outer, block, 2 * inner), jnp.float32)],
+        compiler_params=params(),
+        name="rows_inverse",
+    )(partial, row_tables(outer, inner, length), jnp.asarray(matrix))
+
+
+def ring(axis):
+    devices = lax.axis_size(axis)
+    up = [(i, (i + 1) % devices) for i in range(devices)]
+    return up, [(j, i) for i, j in up]
+
+
+def edges(shift_plane, height, dipole):
+    fields = lambda cut: jnp.concatenate([cut(shift_plane), cut(height[None]), cut(dipole[None])], 0)
+    up, down = ring("tr")
+    top = lax.ppermute(fields(lambda x: x[:, -SUB:]), "tr", up)
+    bottom = lax.ppermute(fields(lambda x: x[:, :SUB]), "tr", down)
+
+    def slab(lanes):
+        body = fields(lambda x: x[..., lanes])
+        return jnp.concatenate([top[..., lanes], body, bottom[..., lanes]], 1)
+
+    up, down = ring("tc")
+    left = lax.ppermute(slab(slice(-LANES, None)), "tc", up)
+    right = lax.ppermute(slab(slice(0, LANES)), "tc", down)
+    return top, bottom, left, right
+
+
+def local_kernels(shift_plane, height, dipole):
+    tc = lax.axis_size("tc")
+    rows, cols = height.shape
+    col_outer, col_inner = factors(cols * tc)
+    row_outer, row_inner = factors(rows * lax.axis_size("tr"))
+    kept = col_inner // 2
+    halos = edges(shift_plane, height, dipole)
+    omega = stencil(shift_plane, height, dipole, halos, tc, True)
+    omega = lax.all_to_all(omega, "tc", split_axis=0, concat_axis=0, tiled=True)
+    spectra = row_forward(omega, col_outer, col_inner)
+    spectra = lax.all_to_all(spectra, ("tr", "tc"), split_axis=0, concat_axis=0, tiled=True)
+    unit, base = stencil(shift_plane, height, dipole, halos, tc, False)
+    place = lax.axis_index(("tr", "tc")) * kept + jnp.arange(kept, dtype=jnp.int32)
+    freq_two, nyquist_two = wavenumbers(cols * tc, kept, place)
+    live_two = jnp.where(nyquist_two, 0.0, 1.0)
+    partial = column_middle(spectra, freq_two[None, :], live_two[None, :], row_outer, row_inner)
+    partial = lax.all_to_all(partial, ("tr", "tc"), split_axis=0, concat_axis=0, tiled=True)
+    speed = row_inverse(partial, col_outer, col_inner, tc)
+    speed = lax.all_to_all(speed, "tc", split_axis=0, concat_axis=0, tiled=True)
+    speed = speed.reshape(rows, cols)
+    return (speed[None] * unit, base + 0.5 * speed * speed)
+
+
+def fits(rows, cols, tr, tc):
+    col_outer, col_inner = factors(cols * tc)
+    row_outer, row_inner = factors(rows * tr)
+    peers = tr * tc
+    return (
+        tc > 1
+        and col_outer == row_outer == peers == 16
+        and col_inner // 2 == LANES
+        and rows // tc == row_inner
+        and rows % (SUB * tc) == 0
+        and col_outer % tc == 0
+    )
+
+
 def solution(mesh):
     in_specs = (
         P(None, ("groups", "tr"), "tc"),
@@ -239,4 +726,11 @@
         P(("groups", "tr"), "tc"),
     )
     out_specs = (P(None, ("groups", "tr"), "tc"), P(("groups", "tr"), "tc"))
-    return jax.shard_map(local, mesh=mesh, in_specs=in_specs, out_specs=out_specs, check_vma=False)
+
+    def chosen(shift_plane, height, dipole):
+        rows, cols = height.shape
+        if fits(rows, cols, lax.axis_size("tr"), lax.axis_size("tc")):
+            return local_kernels(shift_plane, height, dipole)
+        return local(shift_plane, height, dipole)
+
+    return jax.shard_map(chosen, mesh=mesh, in_specs=in_specs, out_specs=out_specs, check_vma=False)

time: 746 us -> 494 us (0.66); the launches traced: 736 us -> 494 us
  other arithmetic: 304 us -> 21.3 us
  Pallas kernels: 0 us -> 210 us
  local copies, waits for them, and re-layouts: 110 us -> 8.86 us
  matrix products: 100 us -> 0 us
  waiting for transfers between devices: 183 us -> 208 us
  blocking collectives: 18.8 us -> 31 us
    pallas_call x0 -> x5, Pallas kernels: none -> 210 us  [the longest x2 134 us: stencil(): pl.pallas_call(kernel, grid=(steps,), in_specs=pair + plane * (count - 2)...]
    div x9 -> x0, other arithmetic: 179 us -> none  [the longest x2 58.6 us: rows_first(): (field[..., :-4, :] - 8.0 * field[..., 1:-3, :] + 8.0 * field[..., 3:-1,...]
    dot_general x8 -> x0, matrix products: 100 us -> none  [the longest x2 41.6 us: forward(): jnp.einsum('s...cb,tsbd->t...cd', sheet_portion, rotation(cos_inner, sin_...]
    concatenate x2 -> x4, other arithmetic: 40.4 us -> 0.18 us  [the longest x2 0.14 us: slab(): return jnp.concatenate([top[..., lanes], body, bottom[..., lanes]], 1)]
    another operation x4 -> x0, local copies, waits for them, and re-layouts: 34.9 us -> none  [the longest x2 15.8 us: twisted(): return jnp.stack([twist_re, twist_im])]
    add x5 -> x1, other arithmetic: 41.5 us -> 6.77 us  [local_kernels(): return (speed[None] * unit, base + 0.5 * speed * speed)]
    another operation x10 -> x0, other arithmetic: 28 us -> none  [the longest x4 14.1 us: twisted(): return jnp.stack([twist_re, twist_im])]
    concatenate x1 -> x0, local copies, waits for them, and re-layouts: 22 us -> none  [padded_2(): x = jnp.concatenate([before, x, after], axis=dim)]
  transfers between devices with their start and end apart: 6 -> 6, of which waited for: 4 -> 6; matrix products, arithmetic and copies ran while one was open for 13% -> 1% of each run, Pallas kernels for 0% -> 16%
where the time goes in v1:
time: 494 us
  Pallas kernels  210 us (43%)
  waiting for transfers between devices  208 us (42%)
  blocking collectives  31 us (6%)
  other arithmetic  21.3 us (4%)
  starting transfers between devices  13.5 us (3%)
  local copies, waits for them, and re-layouts  8.86 us (2%)
    all_to_all x1, waiting for transfers between devices, local_kernels(): lax.all_to_all(spectra, ('tr', 'tc'), split_axis=0, concat_axis=0, tiled=...  181 us
    pallas_call x2, Pallas kernels, stencil(): pl.pallas_call(kernel, grid=(steps,), in_specs=pair + plane * (count - 2)...  134 us
    pallas_call x1, Pallas kernels, column_middle(): pl.pallas_call(kernel, out_shape=jax.ShapeDtypeStruct((outer, 2, inner, w...  32.8 us
    pallas_call x1, Pallas kernels, row_forward(): pl.pallas_call(kernel, grid=(2, rows // block), in_specs=[pl.BlockSpec((t...  27.9 us
    all_to_all x1, blocking collectives, local_kernels(): omega = lax.all_to_all(omega, 'tc', split_axis=0, concat_axis=0, tiled=True)  18.5 us
    pallas_call x1, Pallas kernels, row_inverse(): pl.pallas_call(kernel, grid=(rows // block,), in_specs=[pl.BlockSpec((out...  15.3 us
    mul x1, other arithmetic, local_kernels(): return (speed[None] * unit, base + 0.5 * speed * speed)  13.8 us
    all_to_all x1, waiting for transfers between devices, local_kernels(): lax.all_to_all(partial, ('tr', 'tc'), split_axis=0, concat_axis=0, tiled=...  13.1 us
  transfers between devices with their start and end apart: 6, of which 6 were waited for; matrix products, arithmetic and copies ran while one was open for 1% of the time, Pallas kernels for 16%

profile of v1, /device:TPU:21, one launch (start us, length us, event | category | flops | bytes accessed | tf_op | source)
XLA Modules:
  0.0 493.6 jit_solution(6650919878096278659)
XLA Ops:
  0.6 1.0 fusion.6
  1.6 1.0 fusion.9
  2.6 1.3 collective-permute-start
  3.9 1.2 collective-permute-start.1
  5.1 1.3 fusion.7
  6.4 1.3 fusion.5
  7.7 6.8 %collective-permute-done.refs_9_.refs_6_ = f32[4,8,2048]{2,1,0:T(8,128)S(1)} collective-permute-done((f32[4,8,2048]{2,1,0:T(8,128)S(1)}, f32[4,8,2048]{2,1,0:T(8,128)S(1)}, u32[]{:S(2)}, u32[]{:S(2)}) %collective-permute-start) | collective-permute-done | bytes 262176 | tf_op jit(solution)/shard_map/ppermute | solution.py:672
  14.5 0.0 copy-start.2
  14.5 2.9 collective-permute-done.1.refs_10_.refs_7_
  17.4 0.0 copy-start.3
  17.4 0.1 pad_maximum_fusion
  17.5 0.6 collective-permute-start.2
  18.0 0.1 pad_maximum_fusion.1
  18.1 0.1 collective-permute-start.3
  18.2 2.2 collective-permute-done.2.refs_11_.refs_8_
  20.4 0.0 copy-start
  20.4 1.5 collective-permute-done.3.refs_12_.refs_9_
  21.9 0.0 copy-done.2
  21.9 0.0 copy-done.3
  21.9 0.0 copy-done
  21.9 0.0 copy-start.1
  21.9 1.0 copy-done.1
  22.9 55.2 %omega.1 = f32[2,2,256,2048]{3,2,1,0:T(8,128)} custom-call(f32[2,512,2048]{2,1,0:T(8,128)} %refs_2_.3, f32[2,512,2048]{2,1,0:T(8,128)} %refs_2_.3, f32[2,512,2048]{2,1,0:T(8,128)} %refs_2_.3, f32[512,2048]{1,0:T(8,128)} %refs_5_.3, f32[512,2048]{1,0:T(8,128)} %refs_5_.3, f32[512,2048]{1,0:T(8,128)} %refs_5_.3, f32[512,2048]{1,0:T(8,128)} %refs_8_.1, ...), custom_call_target="tpu_custom_call" | custom-call | tf_op jit(solution)/shard_map/omega/pallas_call | solution.py:454
  78.2 0.0 copy-start.4
  78.2 18.5 %all_to_all.20.x_ref = f32[2,2,256,2048]{3,2,1,0:T(8,128)} all-to-all(f32[2,2,256,2048]{3,2,1,0:T(8,128)} %omega.1), channel_id=1, replica_groups=mesh['groups'=2,'tr'=8,'tc'=2] {'tc'}, dimensions={0} | all-to-all | bytes 16777216 | tf_op jit(solution)/shard_map/all_to_all | solution.py:693
  96.7 0.0 copy-done.4
  96.7 0.7 broadcast_in_dim.20.tw_ref
  97.4 27.9 %rows_forward.1 = f32[16,2,2,256,128]{4,3,2,1,0:T(8,128)} custom-call(f32[2,2,256,2048]{3,2,1,0:T(8,128)} %all_to_all.20.x_ref, f32[2,16,8,256]{3,2,1,0:T(8,128)} %broadcast_in_dim.20.tw_ref, bf16[2,512,256]{2,1,0:T(8,128)(2,1)} %constant.63.clone.m_ref), custom_call_target="tpu_custom_call" | custom-call | tf_op jit(solution)/shard_map/rows_forward/pallas_call | solution.py:515
  125.3 5.3 %all-to-all-start.1 = ((f32[16,2,2,256,128]{4,3,2,1,0:T(8,128)}), f32[16,2,2,256,128]{4,3,2,1,0:T(8,128)}, u32[]{:S(2)}, u32[]{:S(2)}) async-start(f32[16,2,2,256,128]{4,3,2,1,0:T(8,128)} %rows_forward.1), calls=%async_computation.1 | async-start | bytes 16777216 | tf_op jit(solution)/shard_map/all_to_all | solution.py:695
  130.6 0.6 compare_select_fusion.1
  131.2 181.4 %all-to-all-done.1.x_ref = f32[16,2,2,256,128]{4,3,2,1,0:T(8,128)} async-done(((f32[16,2,2,256,128]{4,3,2,1,0:T(8,128)}), f32[16,2,2,256,128]{4,3,2,1,0:T(8,128)}, u32[]{:S(2)}, u32[]{:S(2)}) %all-to-all-start.1) | async-done | bytes 8388640 | tf_op jit(solution)/shard_map/all_to_all | solution.py:695
  312.6 2.6 broadcast_in_dim.21.tw_ref
  315.2 32.8 %columns.1 = f32[16,2,256,128]{3,2,1,0:T(8,128)} custom-call(f32[16,2,2,256,128]{4,3,2,1,0:T(8,128)} %all-to-all-done.1.x_ref, f32[2,16,256,128]{3,2,1,0:T(8,128)} %broadcast_in_dim.21.tw_ref, bf16[2,512,256]{2,1,0:T(8,128)(2,1)} %constant.64.clone.m_ref, f32[1,128]{1,0:T(1,128)} %get-tuple-element.27.f_ref, f32[1,128]{1,0:T(1,128)} %get-tuple-element.26.live_ref), custom_call_target="tpu_custom_call" | custom-call | tf_op jit(solution)/shard_map/columns/pallas_call | solution.py:596
  348.0 5.2 %all-to-all-start.2 = ((f32[16,2,256,128]{3,2,1,0:T(8,128)}), f32[16,2,256,128]{3,2,1,0:T(8,128)}, u32[]{:S(2)}, u32[]{:S(2)}) async-start(f32[16,2,256,128]{3,2,1,0:T(8,128)} %columns.1), calls=%async_computation.2 | async-start | bytes 8388608 | tf_op jit(solution)/shard_map/all_to_all | solution.py:701
  353.2 79.0 %geometry.1 = (f32[3,512,2048]{2,1,0:T(8,128)}, f32[512,2048]{1,0:T(8,128)}) custom-call(f32[2,512,2048]{2,1,0:T(8,128)} %refs_2_.3, f32[2,512,2048]{2,1,0:T(8,128)} %refs_2_.3, f32[2,512,2048]{2,1,0:T(8,128)} %refs_2_.3, f32[512,2048]{1,0:T(8,128)} %refs_5_.3, f32[512,2048]{1,0:T(8,128)} %refs_5_.3, f32[512,2048]{1,0:T(8,128)} %refs_5_.3, ...), custom_call_target="tpu_custom_call" | custom-call | tf_op jit(solution)/shard_map/geometry/pallas_call | solution.py:454
  432.2 13.1 %all-to-all-done.2.x_ref = f32[16,2,256,128]{3,2,1,0:T(8,128)} async-done(((f32[16,2,256,128]{3,2,1,0:T(8,128)}), f32[16,2,256,128]{3,2,1,0:T(8,128)}, u32[]{:S(2)}, u32[]{:S(2)}) %all-to-all-start.2) | async-done | bytes 4194336 | tf_op jit(solution)/shard_map/all_to_all | solution.py:701
  445.2 15.3 %rows_inverse.1 = f32[2,256,2048]{2,1,0:T(8,128)} custom-call(f32[16,2,256,128]{3,2,1,0:T(8,128)} %all-to-all-done.2.x_ref, f32[2,16,8,256]{3,2,1,0:T(8,128)} %broadcast_in_dim.20.tw_ref, bf16[2,256,512]{2,1,0:T(8,128)(2,1)} %constant.65.clone.m_ref), custom_call_target="tpu_custom_call" | custom-call | tf_op jit(solution)/shard_map/rows_inverse/pallas_call | solution.py:647
  460.5 12.5 %all_to_all.21 = f32[2,256,2048]{2,1,0:T(8,128)} all-to-all(f32[2,256,2048]{2,1,0:T(8,128)} %rows_inverse.1), channel_id=1, replica_groups=mesh['groups'=2,'tr'=8,'tc'=2] {'tc'}, dimensions={0} | all-to-all | bytes 8388608 | tf_op jit(solution)/shard_map/all_to_all | solution.py:703
  473.0 13.8 %broadcast_multiply_fusion = f32[3,512,2048]{2,1,0:T(8,128)} fusion(f32[3,512,2048]{2,1,0:T(8,128)} %get-tuple-element.4, f32[512,2048]{1,0:T(8,128)} %bitcast.8), kind=kLoop, calls=%fused_computation.1 | loop fusion | flops 3145728 | bytes 29360128 | tf_op jit(solution)/shard_map/mul | solution.py:705
  486.8 6.8 %fusion = f32[512,2048]{1,0:T(8,128)} fusion(f32[512,2048]{1,0:T(8,128)} %get-tuple-element.5, f32[2,256,2048]{2,1,0:T(8,128)} %all_to_all.21), kind=kLoop, calls=%fused_computation.2 | loop fusion | flops 3145728 | bytes 12582912 | tf_op jit(solution)/shard_map/add | solution.py:705
  (4 shorter events, 0.0 us)
Async XLA Ops:
  2.6 11.9 %collective-permute-start = (f32[4,8,2048]{2,1,0:T(8,128)S(1)}, f32[4,8,2048]{2,1,0:T(8,128)S(1)}, u32[]{:S(2)}, u32[]{:S(2)}) collective-permute-start(f32[4,8,2048]{2,1,0:T(8,128)S(1)} %pad_maximum_fusion.2), channel_id=1, source_target_pairs={{0,2},{2,4},{4,6},{6,8},{8,10},{10,12},{12,14},{14,0},{1,3},{3,5},... | collective-permute-start | bytes 786440 | tf_op jit(solution)/shard_map/ppermute | solution.py:672
  3.9 13.5 %collective-permute-start.1 = (f32[4,8,2048]{2,1,0:T(8,128)S(1)}, f32[4,8,2048]{2,1,0:T(8,128)S(1)}, u32[]{:S(2)}, u32[]{:S(2)}) collective-permute-start(f32[4,8,2048]{2,1,0:T(8,128)S(1)} %pad_maximum_fusion.3), channel_id=1, source_target_pairs={{2,0},{4,2},{6,4},{8,6},{10,8},{12,10},{14,12},{0,14},{3,1},{5,3},... | collective-permute-start | bytes 786440 | tf_op jit(solution)/shard_map/ppermute | solution.py:673
  14.5 7.5 %copy-start.2 = (f32[4,8,2048]{2,1,0:T(8,128)}, f32[4,8,2048]{2,1,0:T(8,128)S(1)}, u32[]{:S(2)}) copy-start(f32[4,8,2048]{2,1,0:T(8,128)S(1)} %collective-permute-done.refs_9_.refs_6_) | copy-start | bytes 786436
  17.4 4.5 copy-start.3
  17.5 2.9 collective-permute-start.2
  18.1 3.8 collective-permute-start.3
  20.4 1.6 copy-start
  21.9 1.0 copy-start.1
  78.2 18.5 %copy-start.4 = (f32[2,16,256]{2,1,0:T(8,128)S(1)}, f32[2,16,256]{2,1,0:T(8,128)}, u32[]{:S(2)}) copy-start(f32[2,16,256]{2,1,0:T(8,128)} %constant.62.clone) | copy-start | bytes 98308
  125.3 187.2 %all-to-all-start.1 = ((f32[16,2,2,256,128]{4,3,2,1,0:T(8,128)}), f32[16,2,2,256,128]{4,3,2,1,0:T(8,128)}, u32[]{:S(2)}, u32[]{:S(2)}) async-start(f32[16,2,2,256,128]{4,3,2,1,0:T(8,128)} %rows_forward.1), calls=%async_computation.1 | async-start | bytes 16777216 | tf_op jit(solution)/shard_map/all_to_all | solution.py:695
  348.0 97.2 %all-to-all-start.2 = ((f32[16,2,256,128]{3,2,1,0:T(8,128)}), f32[16,2,256,128]{3,2,1,0:T(8,128)}, u32[]{:S(2)}, u32[]{:S(2)}) async-start(f32[16,2,256,128]{3,2,1,0:T(8,128)} %columns.1), calls=%async_computation.2 | async-start | bytes 8388608 | tf_op jit(solution)/shard_map/all_to_all | solution.py:701

commit v2 on v1

--- a/solution.py
+++ b/solution.py
@@ -322,11 +322,12 @@
     return (re * c - im * s, im * c + re * s)
 
 
-def stencil(shift_plane, height, dipole, halos, tc, want_omega):
+def stencil(shift_plane, height, dipole, halos, tc, want_omega, part, parts, earlier=()):
     rows, cols = height.shape
-    block = min(64, rows // tc)
-    steps = rows // block
-    chunk = min(256, cols)
+    block = min(64, rows // (tc * parts))
+    steps = rows // (block * parts)
+    ahead = part * steps
+    chunk = min(128, cols)
     wide = min(1024, cols)
     groups = block // SUB
     count = 4 if want_omega else 3
@@ -339,8 +340,9 @@
             top, bottom, left, right, omega_ref, pad, slope = refs
         else:
             arrays, refs = (refs[:6], refs[6:])
+            refs = refs[:4] + refs[4 + len(earlier) :]
             top, bottom, left, right, unit_ref, base_ref, pad, slope, bend = refs
-        i = pl.program_id(0)
+        i = pl.program_id(0) + ahead
         for f in range(count):
             trio = arrays[:3] if f < 2 else arrays[3 * (f - 1) : 3 * f]
             take = (lambda r: r[f]) if f < 2 else (lambda r: r[...])
@@ -348,7 +350,7 @@
             pad[f, SUB : SUB + block, LANES : LANES + cols] = take(cur)
             pad[f, 0:SUB, LANES : LANES + cols] = jnp.where(i == 0, top[f], take(prev))
             pad[f, SUB + block :, LANES : LANES + cols] = jnp.where(
-                i == steps - 1, bottom[f], take(nxt)
+                i == steps * parts - 1, bottom[f], take(nxt)
             )
             pad[f, :, 0:LANES] = left[f, pl.ds(pl.multiple_of(i * block, SUB), tall), :]
             pad[f, :, LANES + cols :] = right[f, pl.ds(pl.multiple_of(i * block, SUB), tall), :]
@@ -424,14 +426,16 @@
 
     per = block // SUB
     plane = [
-        pl.BlockSpec((block, cols), lambda i: (i, 0)),
-        pl.BlockSpec((SUB, cols), lambda i: (jnp.maximum(i * per - 1, 0), 0)),
-        pl.BlockSpec((SUB, cols), lambda i: (jnp.minimum((i + 1) * per, last), 0)),
+        pl.BlockSpec((block, cols), lambda i: (i + ahead, 0)),
+        pl.BlockSpec((SUB, cols), lambda i: (jnp.maximum((i + ahead) * per - 1, 0), 0)),
+        pl.BlockSpec((SUB, cols), lambda i: (jnp.minimum((i + ahead + 1) * per, last), 0)),
     ]
     pair = [
-        pl.BlockSpec((2, block, cols), lambda i: (0, i, 0)),
-        pl.BlockSpec((2, SUB, cols), lambda i: (0, jnp.maximum(i * per - 1, 0), 0)),
-        pl.BlockSpec((2, SUB, cols), lambda i: (0, jnp.minimum((i + 1) * per, last), 0)),
+        pl.BlockSpec((2, block, cols), lambda i: (0, i + ahead, 0)),
+        pl.BlockSpec((2, SUB, cols), lambda i: (0, jnp.maximum((i + ahead) * per - 1, 0), 0)),
+        pl.BlockSpec(
+            (2, SUB, cols), lambda i: (0, jnp.minimum((i + ahead + 1) * per, last), 0)
+        ),
     ]
     whole = [pl.BlockSpec(h.shape, lambda i: (0, 0, 0)) for h in halos]
     ins = [shift_plane] * 3 + [height] * 3 + ([dipole] * 3 if want_omega else [])
@@ -442,25 +446,26 @@
     f32 = lambda *dims: jax.ShapeDtypeStruct(dims, jnp.float32)
     if want_omega:
         half = steps // tc
-        out_shape = f32(tc, 2, rows // tc, cols)
+        out_shape = f32(tc, 2, rows // (tc * parts), cols)
         out_specs = pl.BlockSpec((1, 2, block, cols), lambda i: (i // half, 0, i % half, 0))
     else:
         out_shape = (f32(3, rows, cols), f32(rows, cols))
         out_specs = (
-            pl.BlockSpec((3, block, cols), lambda i: (0, i, 0)),
-            pl.BlockSpec((block, cols), lambda i: (i, 0)),
+            pl.BlockSpec((3, block, cols), lambda i: (0, i + ahead, 0)),
+            pl.BlockSpec((block, cols), lambda i: (i + ahead, 0)),
         )
         scratch.append(pltpu.VMEM((count, tall, cols), jnp.float32))
     return pl.pallas_call(
         kernel,
         grid=(steps,),
-        in_specs=pair + plane * (count - 2) + whole,
+        in_specs=pair + plane * (count - 2) + whole + [pl.BlockSpec(memory_space=pl.ANY)] * len(earlier),
         out_specs=out_specs,
         out_shape=out_shape,
         scratch_shapes=scratch,
         compiler_params=params(),
+        input_output_aliases={len(ins) + 4 + k: k for k in range(len(earlier))},
         name="omega" if want_omega else "geometry",
-    )(*ins, *halos)
+    )(*ins, *halos, *earlier)
 
 
 def row_tables(outer, inner, length):
@@ -528,20 +533,33 @@
     )(omega, row_tables(outer, inner, length), jnp.asarray(matrix))
 
 
-def column_middle(spectra, freq_two, live_two, outer, inner):
+def column_table(outer, inner, width):
+    c, s = unit_circle(outer, inner, outer * inner)
+    table = jnp.asarray(np.stack([c, s]).astype(np.float32))
+    return jnp.broadcast_to(table[..., None], (2, outer, inner, width))
+
+
+def column_middle(spectra, table, freq_two, live_two, outer, inner):
     length = outer * inner
-    width = spectra.shape[-1]
-    c, s = unit_circle(outer, inner, length)
-    table = jnp.asarray(np.stack([c, s]).astype(np.float32))
-    table = jnp.broadcast_to(table[..., None], (2, outer, inner, width))
+    parts = len(spectra)
+    short, width = spectra[0].shape[-2:]
+    tc = inner // short
     c, s = unit_circle(inner, inner, inner)
     matrix = two_halves(np.concatenate([c, s], 0))
 
-    def kernel(x_ref, tw_ref, m_ref, f_ref, live_ref, out_ref, mid):
+    def kernel(*refs):
+        x_refs, refs = (refs[:parts], refs[parts:])
+        tw_ref, m_ref, f_ref, live_ref, out_ref, mid = refs
+
         def down(g, carry):
             r = pl.ds(pl.multiple_of(g * SUB, SUB), SUB)
+            core = g // (short // SUB)
+            t = pl.ds(pl.multiple_of(g % (short // SUB) * SUB, SUB), SUB)
             for p in range(2):
-                z = [(x_ref[a, 0, p, r, :], x_ref[a, 1, p, r, :]) for a in range(outer)]
+                z = []
+                for a in range(outer):
+                    ref, peer = (x_refs[a % parts], a // parts * tc + core)
+                    z.append((ref[peer, 0, p, t, :], ref[peer, 1, p, t, :]))
                 z = butterflies(z, 1.0)
                 for k in range(outer):
                     re, im = z[k] if k == 0 else twist(z[k], tw_ref[0, k, r], tw_ref[1, k, r], 1.0)
@@ -599,7 +617,7 @@
         scratch_shapes=[pltpu.VMEM((outer, inner, 4 * width), jnp.float32)],
         compiler_params=params(),
         name="columns",
-    )(spectra, table, jnp.asarray(matrix), freq_two, live_two)
+    )(*spectra, table, jnp.asarray(matrix), freq_two, live_two)
 
 
 def row_inverse(partial, outer, inner, tc):
@@ -689,15 +707,28 @@
     row_outer, row_inner = factors(rows * lax.axis_size("tr"))
     kept = col_inner // 2
     halos = edges(shift_plane, height, dipole)
-    omega = stencil(shift_plane, height, dipole, halos, tc, True)
-    omega = lax.all_to_all(omega, "tc", split_axis=0, concat_axis=0, tiled=True)
-    spectra = row_forward(omega, col_outer, col_inner)
-    spectra = lax.all_to_all(spectra, ("tr", "tc"), split_axis=0, concat_axis=0, tiled=True)
-    unit, base = stencil(shift_plane, height, dipole, halos, tc, False)
+    parts = rows // row_inner
+    spectra = []
+    charge = dipole
+    for part in range(parts):
+        omega = stencil(shift_plane, height, charge, halos, tc, True, part, parts)
+        omega = lax.all_to_all(omega, "tc", split_axis=0, concat_axis=0, tiled=True)
+        block = row_forward(omega, col_outer, col_inner)
+        block, charge = lax.optimization_barrier((block, dipole))
+        block = lax.all_to_all(block, ("tr", "tc"), split_axis=0, concat_axis=0, tiled=True)
+        spectra.append(block)
+    planes = stencil(shift_plane, height, dipole, halos, tc, False, 0, parts)
     place = lax.axis_index(("tr", "tc")) * kept + jnp.arange(kept, dtype=jnp.int32)
     freq_two, nyquist_two = wavenumbers(cols * tc, kept, place)
     live_two = jnp.where(nyquist_two, 0.0, 1.0)
-    partial = column_middle(spectra, freq_two[None, :], live_two[None, :], row_outer, row_inner)
+    table = column_table(row_outer, row_inner, kept)
+    spectra, planes, table = lax.optimization_barrier((spectra, planes, table))
+    partial = column_middle(
+        spectra, table, freq_two[None, :], live_two[None, :], row_outer, row_inner
+    )
+    for part in range(1, parts):
+        planes = stencil(shift_plane, height, dipole, halos, tc, False, part, parts, planes)
+    unit, base = planes
     partial = lax.all_to_all(partial, ("tr", "tc"), split_axis=0, concat_axis=0, tiled=True)
     speed = row_inverse(partial, col_outer, col_inner, tc)
     speed = lax.all_to_all(speed, "tc", split_axis=0, concat_axis=0, tiled=True)
@@ -714,6 +745,7 @@
         and col_outer == row_outer == peers == 16
         and col_inner // 2 == LANES
         and rows // tc == row_inner
+        and rows % (tc * tc * SUB) == 0
         and rows % (SUB * tc) == 0
         and col_outer % tc == 0
     )

time: 494 us -> 499 us (1.010)
  waiting for transfers between devices: 208 us -> 194 us
  Pallas kernels: 210 us -> 218 us
  blocking collectives: 31 us -> 36.2 us
  starting transfers between devices: 13.5 us -> 18.7 us
    all_to_all x1 -> x2, waiting for transfers between devices: 181 us -> 129 us  [local_kernels(): lax.all_to_all(block, ('tr', 'tc'), split_axis=0, concat_axis=0, tiled=True)]
    all_to_all x1, waiting for transfers between devices: 13.1 us -> 52.3 us  [local_kernels(): lax.all_to_all(partial, ('tr', 'tc'), split_axis=0, concat_axis=0, tiled=...]
    all_to_all x1 -> x2, blocking collectives: 18.5 us -> 23.8 us  [local_kernels(): omega = lax.all_to_all(omega, 'tc', split_axis=0, concat_axis=0, tiled=True)]
    all_to_all x1 -> x2, starting transfers between devices: 5.27 us -> 10.4 us  [local_kernels(): lax.all_to_all(block, ('tr', 'tc'), split_axis=0, concat_axis=0, tiled=True)]
    pallas_call x2 -> x4, Pallas kernels: 134 us -> 139 us  [stencil(): pl.pallas_call(kernel, grid=(steps,), in_specs=pair + plane * (count - 2)...]
    pallas_call x1 -> x2, Pallas kernels: 27.9 us -> 30.3 us  [row_forward(): pl.pallas_call(kernel, grid=(2, rows // block), in_specs=[pl.BlockSpec((t...]
  transfers between devices with their start and end apart: 6 -> 7, of which waited for: 6 -> 7; matrix products, arithmetic and copies ran while one was open for 1% -> 1% of each run, Pallas kernels for 16% -> 19%
where the time goes in v2:
time: 499 us; the launch traced here: 498 us
  Pallas kernels  218 us (44%)
  waiting for transfers between devices  194 us (39%)
  blocking collectives  36.2 us (7%)
  other arithmetic  21.3 us (4%)
  starting transfers between devices  18.7 us (4%)
  local copies, waits for them, and re-layouts  8.75 us (2%)
    pallas_call x4, Pallas kernels, stencil(): pl.pallas_call(kernel, grid=(steps,), in_specs=pair + plane * (count - 2)...  139 us
    all_to_all x2, waiting for transfers between devices, local_kernels(): lax.all_to_all(block, ('tr', 'tc'), split_axis=0, concat_axis=0, tiled=True)  129 us
    all_to_all x1, waiting for transfers between devices, local_kernels(): lax.all_to_all(partial, ('tr', 'tc'), split_axis=0, concat_axis=0, tiled=...  52.3 us
    pallas_call x1, Pallas kernels, column_middle(): pl.pallas_call(kernel, out_shape=jax.ShapeDtypeStruct((outer, 2, inner, w...  33.1 us
    pallas_call x2, Pallas kernels, row_forward(): pl.pallas_call(kernel, grid=(2, rows // block), in_specs=[pl.BlockSpec((t...  30.3 us
    all_to_all x2, blocking collectives, local_kernels(): omega = lax.all_to_all(omega, 'tc', split_axis=0, concat_axis=0, tiled=True)  23.8 us
    pallas_call x1, Pallas kernels, row_inverse(): pl.pallas_call(kernel, grid=(rows // block,), in_specs=[pl.BlockSpec((out...  15.2 us
    mul x1, other arithmetic, local_kernels(): return (speed[None] * unit, base + 0.5 * speed * speed)  13.8 us
  transfers between devices with their start and end apart: 7, of which 7 were waited for; matrix products, arithmetic and copies ran while one was open for 1% of the time, Pallas kernels for 19%

profile of v2, /device:TPU:21, one launch (start us, length us, event | category | flops | bytes accessed | tf_op | source)
XLA Modules:
  0.0 497.8 jit_solution(5412880694316734646)
XLA Ops:
  0.6 1.0 fusion.6
  1.6 1.0 fusion.9
  2.6 1.3 collective-permute-start
  3.9 1.2 collective-permute-start.1
  5.1 1.3 fusion.7
  6.4 1.3 fusion.5
  7.7 6.8 %collective-permute-done.refs_9_.refs_6_ = f32[4,8,2048]{2,1,0:T(8,128)S(1)} collective-permute-done((f32[4,8,2048]{2,1,0:T(8,128)S(1)}, f32[4,8,2048]{2,1,0:T(8,128)S(1)}, u32[]{:S(2)}, u32[]{:S(2)}) %collective-permute-start) | collective-permute-done | bytes 262176 | tf_op jit(solution)/shard_map/ppermute | solution.py:690
  14.5 0.0 copy-start.2
  14.5 2.9 collective-permute-done.1.refs_10_.refs_7_
  17.4 0.0 copy-start.3
  17.4 0.1 pad_maximum_fusion
  17.5 0.6 collective-permute-start.2
  18.0 0.1 pad_maximum_fusion.1
  18.1 0.1 collective-permute-start.3
  18.2 2.2 collective-permute-done.2.refs_11_.refs_8_
  20.4 0.0 copy-start
  20.4 1.5 collective-permute-done.3.refs_12_.refs_9_
  21.9 0.0 copy-done.2
  21.9 0.0 copy-done.3
  21.9 0.0 copy-done
  21.9 0.0 copy-start.1
  21.9 1.0 copy-done.1
  22.9 29.7 %omega.2 = f32[2,2,128,2048]{3,2,1,0:T(8,128)} custom-call(f32[2,512,2048]{2,1,0:T(8,128)} %refs_2_.7, f32[2,512,2048]{2,1,0:T(8,128)} %refs_2_.7, f32[2,512,2048]{2,1,0:T(8,128)} %refs_2_.7, f32[512,2048]{1,0:T(8,128)} %refs_5_.7, f32[512,2048]{1,0:T(8,128)} %refs_5_.7, f32[512,2048]{1,0:T(8,128)} %refs_5_.7, f32[512,2048]{1,0:T(8,128)} %refs_8_.2, ...), custom_call_target="tpu_custom_call" | custom-call | tf_op jit(solution)/shard_map/omega/pallas_call | solution.py:458
  52.7 0.0 copy-start.4
  52.7 11.9 %all_to_all.30.x_ref = f32[2,2,128,2048]{3,2,1,0:T(8,128)} all-to-all(f32[2,2,128,2048]{3,2,1,0:T(8,128)} %omega.2), channel_id=1, replica_groups=mesh['groups'=2,'tr'=8,'tc'=2] {'tc'}, dimensions={0} | all-to-all | bytes 8388608 | tf_op jit(solution)/shard_map/all_to_all | solution.py:715
  64.5 0.0 copy-done.4
  64.5 0.7 broadcast_in_dim.22.tw_ref
  65.2 15.1 %rows_forward.2 = f32[16,2,2,128,128]{4,3,2,1,0:T(8,128)} custom-call(f32[2,2,128,2048]{3,2,1,0:T(8,128)} %all_to_all.30.x_ref, f32[2,16,8,256]{3,2,1,0:T(8,128)} %broadcast_in_dim.22.tw_ref, bf16[2,512,256]{2,1,0:T(8,128)(2,1)} %constant.63.clone.m_ref), custom_call_target="tpu_custom_call" | custom-call | tf_op jit(solution)/shard_map/rows_forward/pallas_call | solution.py:520
  80.4 29.8 %omega.3 = f32[2,2,128,2048]{3,2,1,0:T(8,128)} custom-call(f32[2,512,2048]{2,1,0:T(8,128)} %refs_2_.7, f32[2,512,2048]{2,1,0:T(8,128)} %refs_2_.7, f32[2,512,2048]{2,1,0:T(8,128)} %refs_2_.7, f32[512,2048]{1,0:T(8,128)} %refs_5_.7, f32[512,2048]{1,0:T(8,128)} %refs_5_.7, f32[512,2048]{1,0:T(8,128)} %refs_5_.7, f32[512,2048]{1,0:T(8,128)} %refs_8_.2, ...), custom_call_target="tpu_custom_call" | custom-call | tf_op jit(solution)/shard_map/omega/pallas_call | solution.py:458
  110.1 11.9 %all_to_all.31.x_ref = f32[2,2,128,2048]{3,2,1,0:T(8,128)} all-to-all(f32[2,2,128,2048]{3,2,1,0:T(8,128)} %omega.3), channel_id=1, replica_groups=mesh['groups'=2,'tr'=8,'tc'=2] {'tc'}, dimensions={0} | all-to-all | bytes 8388608 | tf_op jit(solution)/shard_map/all_to_all | solution.py:715
  122.0 5.3 %all-to-all-start.1 = ((f32[16,2,2,128,128]{4,3,2,1,0:T(8,128)}), f32[16,2,2,128,128]{4,3,2,1,0:T(8,128)}, u32[]{:S(2)}, u32[]{:S(2)}) async-start(f32[16,2,2,128,128]{4,3,2,1,0:T(8,128)} %rows_forward.2), calls=%async_computation.1 | async-start | bytes 8388608 | tf_op jit(solution)/shard_map/all_to_all | solution.py:718
  127.3 15.2 %rows_forward.3 = f32[16,2,2,128,128]{4,3,2,1,0:T(8,128)} custom-call(f32[2,2,128,2048]{3,2,1,0:T(8,128)} %all_to_all.31.x_ref, f32[2,16,8,256]{3,2,1,0:T(8,128)} %broadcast_in_dim.22.tw_ref, bf16[2,512,256]{2,1,0:T(8,128)(2,1)} %constant.63.clone.m_ref), custom_call_target="tpu_custom_call" | custom-call | tf_op jit(solution)/shard_map/rows_forward/pallas_call | solution.py:520
  142.5 76.9 %all-to-all-done.1.refs_0_ = f32[16,2,2,128,128]{4,3,2,1,0:T(8,128)} async-done(((f32[16,2,2,128,128]{4,3,2,1,0:T(8,128)}), f32[16,2,2,128,128]{4,3,2,1,0:T(8,128)}, u32[]{:S(2)}, u32[]{:S(2)}) %all-to-all-start.1) | async-done | bytes 4194336 | tf_op jit(solution)/shard_map/all_to_all | solution.py:718
  219.4 5.2 %all-to-all-start.3 = ((f32[16,2,2,128,128]{4,3,2,1,0:T(8,128)}), f32[16,2,2,128,128]{4,3,2,1,0:T(8,128)}, u32[]{:S(2)}, u32[]{:S(2)}) async-start(f32[16,2,2,128,128]{4,3,2,1,0:T(8,128)} %rows_forward.3), calls=%async_computation.3 | async-start | bytes 8388608 | tf_op jit(solution)/shard_map/all_to_all | solution.py:718
  224.6 0.6 compare_select_fusion.1
  225.2 39.8 %geometry.2 = (f32[3,512,2048]{2,1,0:T(8,128)}, f32[512,2048]{1,0:T(8,128)}) custom-call(f32[2,512,2048]{2,1,0:T(8,128)} %refs_2_.7, f32[2,512,2048]{2,1,0:T(8,128)} %refs_2_.7, f32[2,512,2048]{2,1,0:T(8,128)} %refs_2_.7, f32[512,2048]{1,0:T(8,128)} %refs_5_.7, f32[512,2048]{1,0:T(8,128)} %refs_5_.7, f32[512,2048]{1,0:T(8,128)} %refs_5_.7, ...), custom_call_target="tpu_custom_call" | custom-call | tf_op jit(solution)/shard_map/geometry/pallas_call | solution.py:458
  265.0 51.7 %all-to-all-done.3.refs_1_ = f32[16,2,2,128,128]{4,3,2,1,0:T(8,128)} async-done(((f32[16,2,2,128,128]{4,3,2,1,0:T(8,128)}), f32[16,2,2,128,128]{4,3,2,1,0:T(8,128)}, u32[]{:S(2)}, u32[]{:S(2)}) %all-to-all-start.3) | async-done | bytes 4194336 | tf_op jit(solution)/shard_map/all_to_all | solution.py:718
  316.6 2.6 broadcast_in_dim.24.refs_2_
  319.2 33.1 %columns.1 = f32[16,2,256,128]{3,2,1,0:T(8,128)} custom-call(f32[16,2,2,128,128]{4,3,2,1,0:T(8,128)} %all-to-all-done.1.refs_0_, f32[16,2,2,128,128]{4,3,2,1,0:T(8,128)} %all-to-all-done.3.refs_1_, f32[2,16,256,128]{3,2,1,0:T(8,128)} %broadcast_in_dim.24.refs_2_, bf16[2,512,256]{2,1,0:T(8,128)(2,1)} %constant.64.clone.refs_3_, ...), custom_call_target="tpu_custom_call" | custom-call | tf_op jit(solution)/shard_map/columns/pallas_call | solution.py:614
  352.3 5.2 %all-to-all-start.4 = ((f32[16,2,256,128]{3,2,1,0:T(8,128)}), f32[16,2,256,128]{3,2,1,0:T(8,128)}, u32[]{:S(2)}, u32[]{:S(2)}) async-start(f32[16,2,256,128]{3,2,1,0:T(8,128)} %columns.1), calls=%async_computation.4 | async-start | bytes 8388608 | tf_op jit(solution)/shard_map/all_to_all | solution.py:732
  357.5 39.8 %geometry.3 = (f32[3,512,2048]{2,1,0:T(8,128)}, f32[512,2048]{1,0:T(8,128)}) custom-call(f32[2,512,2048]{2,1,0:T(8,128)} %refs_2_.7, f32[2,512,2048]{2,1,0:T(8,128)} %refs_2_.7, f32[2,512,2048]{2,1,0:T(8,128)} %refs_2_.7, f32[512,2048]{1,0:T(8,128)} %refs_5_.7, f32[512,2048]{1,0:T(8,128)} %refs_5_.7, ...), custom_call_target="tpu_custom_call", output_to_operand_aliasing={{0}: (10, {}), {1}: (11, {})} | custom-call | tf_op jit(solution)/shard_map/geometry/pallas_call | solution.py:458
  397.3 52.3 %all-to-all-done.4.x_ref = f32[16,2,256,128]{3,2,1,0:T(8,128)} async-done(((f32[16,2,256,128]{3,2,1,0:T(8,128)}), f32[16,2,256,128]{3,2,1,0:T(8,128)}, u32[]{:S(2)}, u32[]{:S(2)}) %all-to-all-start.4) | async-done | bytes 4194336 | tf_op jit(solution)/shard_map/all_to_all | solution.py:732
  449.5 15.2 %rows_inverse.1 = f32[2,256,2048]{2,1,0:T(8,128)} custom-call(f32[16,2,256,128]{3,2,1,0:T(8,128)} %all-to-all-done.4.x_ref, f32[2,16,8,256]{3,2,1,0:T(8,128)} %broadcast_in_dim.22.tw_ref, bf16[2,256,512]{2,1,0:T(8,128)(2,1)} %constant.65.clone.m_ref), custom_call_target="tpu_custom_call" | custom-call | tf_op jit(solution)/shard_map/rows_inverse/pallas_call | solution.py:665
  464.8 12.5 %all_to_all.32 = f32[2,256,2048]{2,1,0:T(8,128)} all-to-all(f32[2,256,2048]{2,1,0:T(8,128)} %rows_inverse.1), channel_id=1, replica_groups=mesh['groups'=2,'tr'=8,'tc'=2] {'tc'}, dimensions={0} | all-to-all | bytes 8388608 | tf_op jit(solution)/shard_map/all_to_all | solution.py:734
  477.2 13.8 %broadcast_multiply_fusion = f32[3,512,2048]{2,1,0:T(8,128)} fusion(f32[3,512,2048]{2,1,0:T(8,128)} %get-tuple-element.24, f32[512,2048]{1,0:T(8,128)} %bitcast.8), kind=kLoop, calls=%fused_computation.1 | loop fusion | flops 3145728 | bytes 29360128 | tf_op jit(solution)/shard_map/mul | solution.py:736
  491.0 6.8 %fusion = f32[512,2048]{1,0:T(8,128)} fusion(f32[512,2048]{1,0:T(8,128)} %get-tuple-element.25, f32[2,256,2048]{2,1,0:T(8,128)} %all_to_all.32), kind=kLoop, calls=%fused_computation.2 | loop fusion | flops 3145728 | bytes 12582912 | tf_op jit(solution)/shard_map/add | solution.py:736
  (4 shorter events, 0.0 us)
Async XLA Ops:
  2.6 11.9 %collective-permute-start = (f32[4,8,2048]{2,1,0:T(8,128)S(1)}, f32[4,8,2048]{2,1,0:T(8,128)S(1)}, u32[]{:S(2)}, u32[]{:S(2)}) collective-permute-start(f32[4,8,2048]{2,1,0:T(8,128)S(1)} %pad_maximum_fusion.2), channel_id=1, source_target_pairs={{0,2},{2,4},{4,6},{6,8},{8,10},{10,12},{12,14},{14,0},{1,3},{3,5},... | collective-permute-start | bytes 786440 | tf_op jit(solution)/shard_map/ppermute | solution.py:690
  3.9 13.5 %collective-permute-start.1 = (f32[4,8,2048]{2,1,0:T(8,128)S(1)}, f32[4,8,2048]{2,1,0:T(8,128)S(1)}, u32[]{:S(2)}, u32[]{:S(2)}) collective-permute-start(f32[4,8,2048]{2,1,0:T(8,128)S(1)} %pad_maximum_fusion.3), channel_id=1, source_target_pairs={{2,0},{4,2},{6,4},{8,6},{10,8},{12,10},{14,12},{0,14},{3,1},{5,3},... | collective-permute-start | bytes 786440 | tf_op jit(solution)/shard_map/ppermute | solution.py:691
  14.5 7.5 %copy-start.2 = (f32[4,8,2048]{2,1,0:T(8,128)}, f32[4,8,2048]{2,1,0:T(8,128)S(1)}, u32[]{:S(2)}) copy-start(f32[4,8,2048]{2,1,0:T(8,128)S(1)} %collective-permute-done.refs_9_.refs_6_) | copy-start | bytes 786436
  17.4 4.5 copy-start.3
  17.5 2.9 collective-permute-start.2
  18.1 3.8 collective-permute-start.3
  20.4 1.6 copy-start
  21.9 1.0 copy-start.1
  52.7 11.9 %copy-start.4 = (f32[2,16,256]{2,1,0:T(8,128)S(1)}, f32[2,16,256]{2,1,0:T(8,128)}, u32[]{:S(2)}) copy-start(f32[2,16,256]{2,1,0:T(8,128)} %constant.62.clone) | copy-start | bytes 98308
  122.0 97.4 %all-to-all-start.1 = ((f32[16,2,2,128,128]{4,3,2,1,0:T(8,128)}), f32[16,2,2,128,128]{4,3,2,1,0:T(8,128)}, u32[]{:S(2)}, u32[]{:S(2)}) async-start(f32[16,2,2,128,128]{4,3,2,1,0:T(8,128)} %rows_forward.2), calls=%async_computation.1 | async-start | bytes 8388608 | tf_op jit(solution)/shard_map/all_to_all | solution.py:718
  219.4 97.2 %all-to-all-start.3 = ((f32[16,2,2,128,128]{4,3,2,1,0:T(8,128)}), f32[16,2,2,128,128]{4,3,2,1,0:T(8,128)}, u32[]{:S(2)}, u32[]{:S(2)}) async-start(f32[16,2,2,128,128]{4,3,2,1,0:T(8,128)} %rows_forward.3), calls=%async_computation.3 | async-start | bytes 8388608 | tf_op jit(solution)/shard_map/all_to_all | solution.py:718
  352.3 97.2 %all-to-all-start.4 = ((f32[16,2,256,128]{3,2,1,0:T(8,128)}), f32[16,2,256,128]{3,2,1,0:T(8,128)}, u32[]{:S(2)}, u32[]{:S(2)}) async-start(f32[16,2,256,128]{3,2,1,0:T(8,128)} %columns.1), calls=%async_computation.4 | async-start | bytes 8388608 | tf_op jit(solution)/shard_map/all_to_all | solution.py:732

commit v3 on v2

--- a/solution.py
+++ b/solution.py
@@ -176,7 +176,7 @@
 
 
 def wavenumbers(length, kept, positions):
-    outer, inner = factors(length)
+    outer, _ = factors(length)
     number = positions // kept + outer * (positions % kept)
     signed = jnp.where(number >= length // 2, number - length, number)
     return (signed.astype(jnp.float32) / length, number == length // 2)
@@ -196,7 +196,7 @@
     col_count = sheet_rows.shape[-1]
     row_count = height.shape[0] * lax.axis_size("tr")
     col_outer, col_inner = factors(col_count)
-    row_outer, row_inner = factors(row_count)
+    _, row_inner = factors(row_count)
     kept = col_inner // 2
     row_spec = forward(sheet_rows, col_count, kept, True)
     stacked = row_spec.reshape((4,) + row_spec.shape[2:])
@@ -549,7 +549,8 @@
 
     def kernel(*refs):
         x_refs, refs = (refs[:parts], refs[parts:])
-        tw_ref, m_ref, f_ref, live_ref, out_ref, mid = refs
+        tw_ref, m_ref, f_ref, live_ref = refs[:4]
+        out_refs, mid = (refs[4:-1], refs[-1])
 
         def down(g, carry):
             r = pl.ds(pl.multiple_of(g * SUB, SUB), SUB)
@@ -597,23 +598,26 @@
 
         lax.fori_loop(0, outer, turn, 0)
 
-        def up(g, carry):
-            r = pl.ds(pl.multiple_of(g * SUB, SUB), SUB)
-            z = []
-            for k in range(outer):
-                v = (mid[k, r, :width], mid[k, r, width : 2 * width])
-                z.append(v if k == 0 else twist(v, tw_ref[0, k, r], tw_ref[1, k, r], -1.0))
-            z = butterflies(z, -1.0)
-            for a in range(outer):
-                out_ref[a, 0, r, :] = z[a][0] * (1.0 / length)
-                out_ref[a, 1, r, :] = z[a][1] * (1.0 / length)
-            return carry
-
-        lax.fori_loop(0, inner // SUB, up, 0)
+        for h, out_ref in enumerate(out_refs):
+
+            def up(g, carry):
+                r = pl.ds(pl.multiple_of(g * SUB + h * length // outer // parts, SUB), SUB)
+                t = pl.ds(pl.multiple_of(g * SUB, SUB), SUB)
+                z = []
+                for k in range(outer):
+                    v = (mid[k, r, :width], mid[k, r, width : 2 * width])
+                    z.append(v if k == 0 else twist(v, tw_ref[0, k, r], tw_ref[1, k, r], -1.0))
+                z = butterflies(z, -1.0)
+                for a in range(outer):
+                    out_ref[a, 0, t, :] = z[a][0] * (1.0 / length)
+                    out_ref[a, 1, t, :] = z[a][1] * (1.0 / length)
+                return carry
+
+            lax.fori_loop(0, inner // parts // SUB, up, 0)
 
     return pl.pallas_call(
         kernel,
-        out_shape=jax.ShapeDtypeStruct((outer, 2, inner, width), jnp.float32),
+        out_shape=[jax.ShapeDtypeStruct((outer, 2, inner // parts, width), jnp.float32)] * parts,
         scratch_shapes=[pltpu.VMEM((outer, inner, 4 * width), jnp.float32)],
         compiler_params=params(),
         name="columns",
@@ -700,6 +704,15 @@
     return top, bottom, left, right
 
 
+def exchange(x, covered):
+    if not covered:
+        return lax.all_to_all(x, "tc", split_axis=0, concat_axis=0, tiled=True)
+    other = 1 - lax.axis_index("tc")
+    sent = lax.dynamic_index_in_dim(x, other, 0, keepdims=True)
+    got = lax.ppermute(sent, "tc", ring("tc")[0])
+    return lax.dynamic_update_slice_in_dim(x, got, other, 0)
+
+
 def local_kernels(shift_plane, height, dipole):
     tc = lax.axis_size("tc")
     rows, cols = height.shape
@@ -712,7 +725,7 @@
     charge = dipole
     for part in range(parts):
         omega = stencil(shift_plane, height, charge, halos, tc, True, part, parts)
-        omega = lax.all_to_all(omega, "tc", split_axis=0, concat_axis=0, tiled=True)
+        omega = exchange(omega, part > 0)
         block = row_forward(omega, col_outer, col_inner)
         block, charge = lax.optimization_barrier((block, dipole))
         block = lax.all_to_all(block, ("tr", "tc"), split_axis=0, concat_axis=0, tiled=True)
@@ -729,11 +742,45 @@
     for part in range(1, parts):
         planes = stencil(shift_plane, height, dipole, halos, tc, False, part, parts, planes)
     unit, base = planes
-    partial = lax.all_to_all(partial, ("tr", "tc"), split_axis=0, concat_axis=0, tiled=True)
-    speed = row_inverse(partial, col_outer, col_inner, tc)
-    speed = lax.all_to_all(speed, "tc", split_axis=0, concat_axis=0, tiled=True)
-    speed = speed.reshape(rows, cols)
-    return (speed[None] * unit, base + 0.5 * speed * speed)
+    results = ()
+    for part in range(parts):
+        block = lax.all_to_all(partial[part], ("tr", "tc"), split_axis=0, concat_axis=0, tiled=True)
+        speed = row_inverse(block, col_outer, col_inner, tc)
+        speed = exchange(speed, part < parts - 1)
+        results = finish(speed, unit, base, part, parts, results)
+    return tuple(results)
+
+
+def finish(speed, unit, base, part, parts, earlier):
+    _, cols = base.shape
+    tc, short, _ = speed.shape
+    block = min(64, short)
+    steps = short // block
+
+    def kernel(s_ref, u_ref, b_ref, *refs):
+        v_ref, d_ref = refs[len(earlier) :]
+        s = s_ref[0]
+        for f in range(3):
+            v_ref[f] = s * u_ref[f]
+        d_ref[...] = b_ref[...] + 0.5 * s * s
+
+    row = lambda t, j: (t * parts + part) * steps + j
+    plane = pl.BlockSpec((block, cols), lambda t, j: (row(t, j), 0))
+    triple = pl.BlockSpec((3, block, cols), lambda t, j: (0, row(t, j), 0))
+    return pl.pallas_call(
+        kernel,
+        grid=(tc, steps),
+        in_specs=[pl.BlockSpec((1, block, cols), lambda t, j: (t, j, 0)), triple, plane]
+        + [pl.BlockSpec(memory_space=pl.ANY)] * len(earlier),
+        out_specs=(triple, plane),
+        out_shape=(
+            jax.ShapeDtypeStruct(unit.shape, jnp.float32),
+            jax.ShapeDtypeStruct(base.shape, jnp.float32),
+        ),
+        input_output_aliases={3 + k: k for k in range(len(earlier))},
+        compiler_params=params(),
+        name="finish",
+    )(speed, unit, base, *earlier)
 
 
 def fits(rows, cols, tr, tc):
@@ -741,7 +788,7 @@
     row_outer, row_inner = factors(rows * tr)
     peers = tr * tc
     return (
-        tc > 1
+        tc == 2
         and col_outer == row_outer == peers == 16
         and col_inner // 2 == LANES
         and rows // tc == row_inner
@@ -765,4 +812,6 @@
             return local_kernels(shift_plane, height, dipole)
         return local(shift_plane, height, dipole)
 
-    return jax.shard_map(chosen, mesh=mesh, in_specs=in_specs, out_specs=out_specs, check_vma=False)
+    return jax.shard_map(
+        chosen, mesh=mesh, in_specs=in_specs, out_specs=out_specs, check_vma=False
+    )

time: 499 us -> 453 us (0.908)
  waiting for transfers between devices: 194 us -> 107 us
  blocking collectives: 36.2 us -> 64 us
  other arithmetic: 21.3 us -> 0.79 us
  Pallas kernels: 218 us -> 235 us
  local copies, waits for them, and re-layouts: 8.75 us -> 18.1 us
  starting transfers between devices: 18.7 us -> 25.3 us
    all_to_all x1 -> x2, waiting for transfers between devices: 52.3 us -> 0.01 us  [the longest x1 0.01 us: local_kernels(): lax.all_to_all(partial[part], ('tr', 'tc'), split_axis=0, concat_axis=0,...]
    all_to_all x2, waiting for transfers between devices: 129 us -> 90.4 us  [local_kernels(): lax.all_to_all(block, ('tr', 'tc'), split_axis=0, concat_axis=0, tiled=True)]
    all_to_all x3 -> x2, blocking collectives: 36.2 us -> 64 us  [the longest x1 52.1 us: local_kernels(): lax.all_to_all(partial[part], ('tr', 'tc'), split_axis=0, concat_axis=0,...]
    pallas_call x1 -> x3, Pallas kernels: 33.1 us -> 48.2 us  [the longest x1 33.2 us: column_middle(): pl.pallas_call(kernel, out_shape=[jax.ShapeDtypeStruct((outer, 2, inner /...]
    mul x1 -> x0, other arithmetic: 13.8 us -> none  [local_kernels(): return (speed[None] * unit, base + 0.5 * speed * speed)]
    add x1 -> x0, other arithmetic: 6.77 us -> none  [local_kernels(): return (speed[None] * unit, base + 0.5 * speed * speed)]
    all_to_all x1 -> x2, starting transfers between devices: 5.16 us -> 10.5 us  [the longest x1 5.48 us: local_kernels(): lax.all_to_all(partial[part], ('tr', 'tc'), split_axis=0, concat_axis=0,...]
    pallas_call x1 -> x2, Pallas kernels: 15.2 us -> 17.6 us  [row_inverse(): pl.pallas_call(kernel, grid=(rows // block,), in_specs=[pl.BlockSpec((out...]
  transfers between devices with their start and end apart: 7 -> 10, of which waited for: 7 -> 7; matrix products, arithmetic and copies ran while one was open for 1% -> 2% of each run, Pallas kernels for 19% -> 33%
where the time goes in v3:
time: 453 us; the launch traced here: 451 us
  Pallas kernels  235 us (52%)
  waiting for transfers between devices  107 us (24%)
  blocking collectives  64 us (14%)
  starting transfers between devices  25.3 us (6%)
  local copies, waits for them, and re-layouts  18.1 us (4%)
    pallas_call x4, Pallas kernels, stencil(): pl.pallas_call(kernel, grid=(steps,), in_specs=pair + plane * (count - 2)...  139 us
    all_to_all x2, waiting for transfers between devices, local_kernels(): lax.all_to_all(block, ('tr', 'tc'), split_axis=0, concat_axis=0, tiled=True)  90.4 us
    all_to_all x1, blocking collectives, local_kernels(): lax.all_to_all(partial[part], ('tr', 'tc'), split_axis=0, concat_axis=0,...  52.1 us
    pallas_call x1, Pallas kernels, column_middle(): pl.pallas_call(kernel, out_shape=[jax.ShapeDtypeStruct((outer, 2, inner /...  33.2 us
    pallas_call x2, Pallas kernels, row_forward(): pl.pallas_call(kernel, grid=(2, rows // block), in_specs=[pl.BlockSpec((t...  30.4 us
    pallas_call x2, Pallas kernels, row_inverse(): pl.pallas_call(kernel, grid=(rows // block,), in_specs=[pl.BlockSpec((out...  17.6 us
    pallas_call x2, Pallas kernels, finish(): pl.pallas_call(kernel, grid=(tc, steps), in_specs=[pl.BlockSpec((1, block...  15 us
    all_to_all x1, blocking collectives, exchange(): return lax.all_to_all(x, 'tc', split_axis=0, concat_axis=0, tiled=True)  11.9 us
  transfers between devices with their start and end apart: 10, of which 7 were waited for; matrix products, arithmetic and copies ran while one was open for 2% of the time, Pallas kernels for 33%

profile of v3, /device:TPU:21, one launch (start us, length us, event | category | flops | bytes accessed | tf_op | source)
XLA Modules:
  0.0 451.4 jit_solution(9935166709691700529)
XLA Ops:
  0.6 1.0 fusion.5
  1.6 1.0 fusion.8
  2.6 1.3 collective-permute-start
  3.9 1.2 collective-permute-start.1
  5.1 1.3 fusion.6
  6.4 1.3 fusion.4
  7.7 6.8 %collective-permute-done.refs_9_.refs_6_ = f32[4,8,2048]{2,1,0:T(8,128)S(1)} collective-permute-done((f32[4,8,2048]{2,1,0:T(8,128)S(1)}, f32[4,8,2048]{2,1,0:T(8,128)S(1)}, u32[]{:S(2)}, u32[]{:S(2)}) %collective-permute-start) | collective-permute-done | bytes 262176 | tf_op jit(solution)/shard_map/ppermute | solution.py:694
  14.5 2.9 collective-permute-done.1.refs_10_.refs_7_
  17.4 0.1 pad_maximum_fusion
  17.5 0.6 collective-permute-start.2
  18.0 0.1 pad_maximum_fusion.1
  18.1 0.5 collective-permute-start.3
  18.6 1.8 collective-permute-done.2.refs_11_.refs_8_
  20.4 1.5 collective-permute-done.3.refs_12_.refs_9_
  21.9 1.0 copy-done.3
  22.9 29.7 %omega.2 = f32[2,2,128,2048]{3,2,1,0:T(8,128)} custom-call(f32[2,512,2048]{2,1,0:T(8,128)} %refs_2_.7, f32[2,512,2048]{2,1,0:T(8,128)} %refs_2_.7, f32[2,512,2048]{2,1,0:T(8,128)} %refs_2_.7, f32[512,2048]{1,0:T(8,128)} %refs_5_.7, f32[512,2048]{1,0:T(8,128)} %refs_5_.7, f32[512,2048]{1,0:T(8,128)} %refs_5_.7, f32[512,2048]{1,0:T(8,128)} %refs_8_.2, ...), custom_call_target="tpu_custom_call" | custom-call | tf_op jit(solution)/shard_map/omega/pallas_call | solution.py:458
  52.7 11.9 %all_to_all.30.x_ref = f32[2,2,128,2048]{3,2,1,0:T(8,128)} all-to-all(f32[2,2,128,2048]{3,2,1,0:T(8,128)} %omega.2), channel_id=1, replica_groups=mesh['groups'=2,'tr'=8,'tc'=2] {'tc'}, dimensions={0} | all-to-all | bytes 8388608 | tf_op jit(solution)/shard_map/all_to_all | solution.py:709
  64.6 0.7 broadcast_in_dim.24.tw_ref
  65.3 15.1 %rows_forward.2 = f32[16,2,2,128,128]{4,3,2,1,0:T(8,128)} custom-call(f32[2,2,128,2048]{3,2,1,0:T(8,128)} %all_to_all.30.x_ref, f32[2,16,8,256]{3,2,1,0:T(8,128)} %broadcast_in_dim.24.tw_ref, bf16[2,512,256]{2,1,0:T(8,128)(2,1)} %constant.73.clone.m_ref), custom_call_target="tpu_custom_call" | custom-call | tf_op jit(solution)/shard_map/rows_forward/pallas_call | solution.py:520
  80.4 5.3 %all-to-all-start.1 = ((f32[16,2,2,128,128]{4,3,2,1,0:T(8,128)}), f32[16,2,2,128,128]{4,3,2,1,0:T(8,128)}, u32[]{:S(2)}, u32[]{:S(2)}) async-start(f32[16,2,2,128,128]{4,3,2,1,0:T(8,128)} %rows_forward.2), calls=%async_computation.1 | async-start | bytes 8388608 | tf_op jit(solution)/shard_map/all_to_all | solution.py:731
  85.7 29.8 %omega.3 = f32[2,2,128,2048]{3,2,1,0:T(8,128)} custom-call(f32[2,512,2048]{2,1,0:T(8,128)} %refs_2_.7, f32[2,512,2048]{2,1,0:T(8,128)} %refs_2_.7, f32[2,512,2048]{2,1,0:T(8,128)} %refs_2_.7, f32[512,2048]{1,0:T(8,128)} %refs_5_.7, f32[512,2048]{1,0:T(8,128)} %refs_5_.7, f32[512,2048]{1,0:T(8,128)} %refs_5_.7, f32[512,2048]{1,0:T(8,128)} %refs_8_.2, ...), custom_call_target="tpu_custom_call" | custom-call | tf_op jit(solution)/shard_map/omega/pallas_call | solution.py:458
  115.4 1.9 constant_dynamic-slice_fusion.1
  117.3 0.5 collective-permute-start.4
  117.8 3.8 collective-permute-done.4
  121.6 0.2 constant_dynamic-update-slice_fusion.1.x_ref
  121.8 0.0 copy-start.1
  121.8 2.0 copy-done.1
  123.8 15.2 %rows_forward.3 = f32[16,2,2,128,128]{4,3,2,1,0:T(8,128)} custom-call(f32[2,2,128,2048]{3,2,1,0:T(8,128)} %copy-done.1, f32[2,16,8,256]{3,2,1,0:T(8,128)} %broadcast_in_dim.24.tw_ref, bf16[2,512,256]{2,1,0:T(8,128)(2,1)} %constant.73.clone.m_ref), custom_call_target="tpu_custom_call" | custom-call | tf_op jit(solution)/shard_map/rows_forward/pallas_call | solution.py:520
  139.1 38.7 %all-to-all-done.1.refs_0_ = f32[16,2,2,128,128]{4,3,2,1,0:T(8,128)} async-done(((f32[16,2,2,128,128]{4,3,2,1,0:T(8,128)}), f32[16,2,2,128,128]{4,3,2,1,0:T(8,128)}, u32[]{:S(2)}, u32[]{:S(2)}) %all-to-all-start.1) | async-done | bytes 4194336 | tf_op jit(solution)/shard_map/all_to_all | solution.py:731
  177.8 5.2 %all-to-all-start.2 = ((f32[16,2,2,128,128]{4,3,2,1,0:T(8,128)}), f32[16,2,2,128,128]{4,3,2,1,0:T(8,128)}, u32[]{:S(2)}, u32[]{:S(2)}) async-start(f32[16,2,2,128,128]{4,3,2,1,0:T(8,128)} %rows_forward.3), calls=%async_computation.2 | async-start | bytes 8388608 | tf_op jit(solution)/shard_map/all_to_all | solution.py:731
  182.9 0.6 compare_select_fusion.1
  183.5 39.8 %geometry.2 = (f32[3,512,2048]{2,1,0:T(8,128)}, f32[512,2048]{1,0:T(8,128)}) custom-call(f32[2,512,2048]{2,1,0:T(8,128)} %refs_2_.7, f32[2,512,2048]{2,1,0:T(8,128)} %refs_2_.7, f32[2,512,2048]{2,1,0:T(8,128)} %refs_2_.7, f32[512,2048]{1,0:T(8,128)} %refs_5_.7, f32[512,2048]{1,0:T(8,128)} %refs_5_.7, f32[512,2048]{1,0:T(8,128)} %refs_5_.7, ...), custom_call_target="tpu_custom_call" | custom-call | tf_op jit(solution)/shard_map/geometry/pallas_call | solution.py:458
  223.3 51.7 %all-to-all-done.2.refs_1_ = f32[16,2,2,128,128]{4,3,2,1,0:T(8,128)} async-done(((f32[16,2,2,128,128]{4,3,2,1,0:T(8,128)}), f32[16,2,2,128,128]{4,3,2,1,0:T(8,128)}, u32[]{:S(2)}, u32[]{:S(2)}) %all-to-all-start.2) | async-done | bytes 4194336 | tf_op jit(solution)/shard_map/all_to_all | solution.py:731
  275.0 2.6 broadcast_in_dim.26.refs_2_
  277.6 33.2 %columns.1 = (f32[16,2,128,128]{3,2,1,0:T(8,128)}, f32[16,2,128,128]{3,2,1,0:T(8,128)}) custom-call(f32[16,2,2,128,128]{4,3,2,1,0:T(8,128)} %all-to-all-done.1.refs_0_, f32[16,2,2,128,128]{4,3,2,1,0:T(8,128)} %all-to-all-done.2.refs_1_, f32[2,16,256,128]{3,2,1,0:T(8,128)} %broadcast_in_dim.26.refs_2_, bf16[2,512,256]{2,1,0:T(8,128)(2,1)} %constant.74.clone.refs_3_, ...), custom_call_target="tpu_custom_call" | custom-call | tf_op jit(solution)/shard_map/columns/pallas_call | solution.py:618
  310.8 52.1 %all_to_all.31.x_ref = f32[16,2,128,128]{3,2,1,0:T(8,128)} all-to-all(f32[16,2,128,128]{3,2,1,0:T(8,128)} %get-tuple-element.31), channel_id=1, replica_groups=mesh['groups'=2,'tr'=8,'tc'=2] {'tr','tc'}, dimensions={0} | all-to-all | bytes 4194304 | tf_op jit(solution)/shard_map/all_to_all | solution.py:747
  362.9 5.5 %all-to-all-start.3 = ((f32[16,2,128,128]{3,2,1,0:T(8,128)}), f32[16,2,128,128]{3,2,1,0:T(8,128)S(1)}, u32[]{:S(2)}, u32[]{:S(2)}) async-start(f32[16,2,128,128]{3,2,1,0:T(8,128)} %get-tuple-element.26), calls=%async_computation.3 | async-start | bytes 4194304 | tf_op jit(solution)/shard_map/all_to_all | solution.py:747
  368.4 8.8 %rows_inverse.3 = f32[2,128,2048]{2,1,0:T(8,128)} custom-call(f32[16,2,128,128]{3,2,1,0:T(8,128)} %all_to_all.31.x_ref, f32[2,16,8,256]{3,2,1,0:T(8,128)} %broadcast_in_dim.24.tw_ref, bf16[2,256,512]{2,1,0:T(8,128)(2,1)} %constant.75.clone.m_ref), custom_call_target="tpu_custom_call" | custom-call | tf_op jit(solution)/shard_map/rows_inverse/pallas_call | solution.py:669
  377.2 2.3 constant_dynamic-slice_fusion
  379.5 0.4 collective-permute-start.5
  379.9 39.9 %geometry.3 = (f32[3,512,2048]{2,1,0:T(8,128)}, f32[512,2048]{1,0:T(8,128)}) custom-call(f32[2,512,2048]{2,1,0:T(8,128)} %refs_2_.7, f32[2,512,2048]{2,1,0:T(8,128)} %refs_2_.7, f32[2,512,2048]{2,1,0:T(8,128)} %refs_2_.7, f32[512,2048]{1,0:T(8,128)} %refs_5_.7, f32[512,2048]{1,0:T(8,128)} %refs_5_.7, ...), custom_call_target="tpu_custom_call", output_to_operand_aliasing={{0}: (10, {}), {1}: (11, {})} | custom-call | tf_op jit(solution)/shard_map/geometry/pallas_call | solution.py:458
  419.8 1.3 copy-done.6
  421.1 8.8 %rows_inverse.2 = f32[2,128,2048]{2,1,0:T(8,128)} custom-call(f32[16,2,128,128]{3,2,1,0:T(8,128)} %copy-done.6, f32[2,16,8,256]{3,2,1,0:T(8,128)} %broadcast_in_dim.24.tw_ref, bf16[2,256,512]{2,1,0:T(8,128)(2,1)} %constant.75.clone.m_ref), custom_call_target="tpu_custom_call" | custom-call | tf_op jit(solution)/shard_map/rows_inverse/pallas_call | solution.py:669
  429.9 5.0 %all-to-all-start.4 = ((f32[2,128,2048]{2,1,0:T(8,128)}), f32[2,128,2048]{2,1,0:T(8,128)}, u32[]{:S(2)}, u32[]{:S(2)}) async-start(f32[2,128,2048]{2,1,0:T(8,128)} %rows_inverse.2), calls=%async_computation.4 | async-start | bytes 4194304 | tf_op jit(solution)/shard_map/all_to_all | solution.py:709
  434.9 0.1 constant_dynamic-update-slice_fusion.s_ref
  435.1 1.4 copy-done.5
  436.4 7.5 %finish.2 = (f32[3,512,2048]{2,1,0:T(8,128)}, f32[512,2048]{1,0:T(8,128)}) custom-call(f32[2,128,2048]{2,1,0:T(8,128)} %copy-done.5, f32[3,512,2048]{2,1,0:T(8,128)} %get-tuple-element.29.u_ref, f32[512,2048]{1,0:T(8,128)} %get-tuple-element.30.b_ref), custom_call_target="tpu_custom_call" | custom-call | tf_op jit(solution)/shard_map/finish/pallas_call | solution.py:770
  443.9 7.5 %finish.3 = (f32[3,512,2048]{2,1,0:T(8,128)}, f32[512,2048]{1,0:T(8,128)}) custom-call(f32[2,128,2048]{2,1,0:T(8,128)} %all-to-all-done.4.s_ref, f32[3,512,2048]{2,1,0:T(8,128)} %get-tuple-element.29.u_ref, f32[512,2048]{1,0:T(8,128)} %get-tuple-element.30.b_ref, ...), custom_call_target="tpu_custom_call", output_to_operand_aliasing={{0}: (3, {}), {1}: (4, {})} | custom-call | tf_op jit(solution)/shard_map/finish/pallas_call | solution.py:770
  (22 shorter events, 0.1 us)
Async XLA Ops:
  2.6 11.9 %collective-permute-start = (f32[4,8,2048]{2,1,0:T(8,128)S(1)}, f32[4,8,2048]{2,1,0:T(8,128)S(1)}, u32[]{:S(2)}, u32[]{:S(2)}) collective-permute-start(f32[4,8,2048]{2,1,0:T(8,128)S(1)} %pad_maximum_fusion.2), channel_id=1, source_target_pairs={{0,2},{2,4},{4,6},{6,8},{8,10},{10,12},{12,14},{14,0},{1,3},{3,5},... | collective-permute-start | bytes 786440 | tf_op jit(solution)/shard_map/ppermute | solution.py:694
  3.9 13.5 %collective-permute-start.1 = (f32[4,8,2048]{2,1,0:T(8,128)S(1)}, f32[4,8,2048]{2,1,0:T(8,128)S(1)}, u32[]{:S(2)}, u32[]{:S(2)}) collective-permute-start(f32[4,8,2048]{2,1,0:T(8,128)S(1)} %pad_maximum_fusion.3), channel_id=1, source_target_pairs={{2,0},{4,2},{6,4},{8,6},{10,8},{12,10},{14,12},{0,14},{3,1},{5,3},... | collective-permute-start | bytes 786440 | tf_op jit(solution)/shard_map/ppermute | solution.py:695
  14.5 3.6 copy-start.7
  17.4 0.7 copy-start.8
  17.5 2.9 collective-permute-start.2
  18.1 3.8 collective-permute-start.3
  20.4 1.5 copy-start.2
  21.9 1.0 copy-start.3
  52.7 11.9 %copy-start.9 = (f32[2,16,256]{2,1,0:T(8,128)S(1)}, f32[2,16,256]{2,1,0:T(8,128)}, u32[]{:S(2)}) copy-start(f32[2,16,256]{2,1,0:T(8,128)} %constant.72.clone) | copy-start | bytes 98308
  80.4 97.3 %all-to-all-start.1 = ((f32[16,2,2,128,128]{4,3,2,1,0:T(8,128)}), f32[16,2,2,128,128]{4,3,2,1,0:T(8,128)}, u32[]{:S(2)}, u32[]{:S(2)}) async-start(f32[16,2,2,128,128]{4,3,2,1,0:T(8,128)} %rows_forward.2), calls=%async_computation.1 | async-start | bytes 8388608 | tf_op jit(solution)/shard_map/all_to_all | solution.py:731
  115.4 6.1 %copy-start = (f32[2,2,128,2048]{3,2,1,0:T(8,128)S(1)}, f32[2,2,128,2048]{3,2,1,0:T(8,128)}, u32[]{:S(2)}) copy-start(f32[2,2,128,2048]{3,2,1,0:T(8,128)} %omega.3) | copy-start | bytes 12582916
  117.3 4.2 collective-permute-start.4
  121.8 2.0 copy-start.1
  177.8 97.2 %all-to-all-start.2 = ((f32[16,2,2,128,128]{4,3,2,1,0:T(8,128)}), f32[16,2,2,128,128]{4,3,2,1,0:T(8,128)}, u32[]{:S(2)}, u32[]{:S(2)}) async-start(f32[16,2,2,128,128]{4,3,2,1,0:T(8,128)} %rows_forward.3), calls=%async_computation.2 | async-start | bytes 8388608 | tf_op jit(solution)/shard_map/all_to_all | solution.py:731
  362.9 56.9 %all-to-all-start.3 = ((f32[16,2,128,128]{3,2,1,0:T(8,128)}), f32[16,2,128,128]{3,2,1,0:T(8,128)S(1)}, u32[]{:S(2)}, u32[]{:S(2)}) async-start(f32[16,2,128,128]{3,2,1,0:T(8,128)} %get-tuple-element.26), calls=%async_computation.3 | async-start | bytes 4194304 | tf_op jit(solution)/shard_map/all_to_all | solution.py:747
  379.5 55.4 %collective-permute-start.5 = (f32[1,128,2048]{2,1,0:T(8,128)}, f32[1,128,2048]{2,1,0:T(8,128)S(1)}, u32[]{:S(2)}, u32[]{:S(2)}) collective-permute-start(f32[1,128,2048]{2,1,0:T(8,128)} %constant_dynamic-slice_fusion), channel_id=1, source_target_pairs={{0,1},{1,0},{2,3},{3,2},{4,5},{5,4},{6,7},{7,6},{8,9},{9,8},{10,11... | collective-permute-start | bytes 3145736 | tf_op jit(solution)/shard_map/ppermute | solution.py:712
  419.8 1.3 copy-start.6
  429.9 5.1 %copy-start.4 = (f32[2,128,2048]{2,1,0:T(8,128)S(1)}, f32[2,128,2048]{2,1,0:T(8,128)}, u32[]{:S(2)}) copy-start(f32[2,128,2048]{2,1,0:T(8,128)} %rows_inverse.3) | copy-start | bytes 6291460
  429.9 14.0 %all-to-all-start.4 = ((f32[2,128,2048]{2,1,0:T(8,128)}), f32[2,128,2048]{2,1,0:T(8,128)}, u32[]{:S(2)}, u32[]{:S(2)}) async-start(f32[2,128,2048]{2,1,0:T(8,128)} %rows_inverse.2), calls=%async_computation.4 | async-start | bytes 4194304 | tf_op jit(solution)/shard_map/all_to_all | solution.py:709
  435.0 1.4 copy-start.5

commit v4 on v3

--- a/solution.py
+++ b/solution.py
@@ -539,36 +539,42 @@
     return jnp.broadcast_to(table[..., None], (2, outer, inner, width))
 
 
-def column_middle(spectra, table, freq_two, live_two, outer, inner):
+def column_middle(spectra, table, freq_two, live_two, outer, inner, tc):
     length = outer * inner
-    parts = len(spectra)
+    pieces = len(spectra)
     short, width = spectra[0].shape[-2:]
-    tc = inner // short
+    sub = inner // (short * tc)
+    parts = pieces // sub
     c, s = unit_circle(inner, inner, inner)
     matrix = two_halves(np.concatenate([c, s], 0))
 
     def kernel(*refs):
-        x_refs, refs = (refs[:parts], refs[parts:])
+        x_refs, refs = (refs[:pieces], refs[pieces:])
         tw_ref, m_ref, f_ref, live_ref = refs[:4]
         out_refs, mid = (refs[4:-1], refs[-1])
 
-        def down(g, carry):
-            r = pl.ds(pl.multiple_of(g * SUB, SUB), SUB)
-            core = g // (short // SUB)
-            t = pl.ds(pl.multiple_of(g % (short // SUB) * SUB, SUB), SUB)
-            for p in range(2):
-                z = []
-                for a in range(outer):
-                    ref, peer = (x_refs[a % parts], a // parts * tc + core)
-                    z.append((ref[peer, 0, p, t, :], ref[peer, 1, p, t, :]))
-                z = butterflies(z, 1.0)
-                for k in range(outer):
-                    re, im = z[k] if k == 0 else twist(z[k], tw_ref[0, k, r], tw_ref[1, k, r], 1.0)
-                    mid[k, r, (2 * p) * width : (2 * p + 1) * width] = re
-                    mid[k, r, (2 * p + 1) * width : (2 * p + 2) * width] = im
-            return carry
-
-        lax.fori_loop(0, inner // SUB, down, 0)
+        for q in range(sub):
+
+            def down(g, carry):
+                r = pl.ds(pl.multiple_of(g * SUB + q * short * tc, SUB), SUB)
+                core = g // (short // SUB)
+                t = pl.ds(pl.multiple_of(g % (short // SUB) * SUB, SUB), SUB)
+                for p in range(2):
+                    z = []
+                    for a in range(outer):
+                        ref, peer = (x_refs[a % parts * sub + q], a // parts * tc + core)
+                        z.append((ref[peer, 0, p, t, :], ref[peer, 1, p, t, :]))
+                    z = butterflies(z, 1.0)
+                    for k in range(outer):
+                        v = z[k]
+                        if k:
+                            v = twist(v, tw_ref[0, k, r], tw_ref[1, k, r], 1.0)
+                        mid[k, r, (2 * p) * width : (2 * p + 1) * width] = v[0]
+                        mid[k, r, (2 * p + 1) * width : (2 * p + 2) * width] = v[1]
+                return carry
+
+            lax.fori_loop(0, short * tc // SUB, down, 0)
+
         fre_two = f_ref[...]
         live_cols = live_ref[...]
         weights = (m_ref[0], m_ref[1])
@@ -704,9 +710,7 @@
     return top, bottom, left, right
 
 
-def exchange(x, covered):
-    if not covered:
-        return lax.all_to_all(x, "tc", split_axis=0, concat_axis=0, tiled=True)
+def exchange(x):
     other = 1 - lax.axis_index("tc")
     sent = lax.dynamic_index_in_dim(x, other, 0, keepdims=True)
     got = lax.ppermute(sent, "tc", ring("tc")[0])
@@ -721,11 +725,12 @@
     kept = col_inner // 2
     halos = edges(shift_plane, height, dipole)
     parts = rows // row_inner
+    pieces = 2 * parts
     spectra = []
     charge = dipole
-    for part in range(parts):
-        omega = stencil(shift_plane, height, charge, halos, tc, True, part, parts)
-        omega = exchange(omega, part > 0)
+    for part in range(pieces):
+        omega = stencil(shift_plane, height, charge, halos, tc, True, part, pieces)
+        omega = exchange(omega)
         block = row_forward(omega, col_outer, col_inner)
         block, charge = lax.optimization_barrier((block, dipole))
         block = lax.all_to_all(block, ("tr", "tc"), split_axis=0, concat_axis=0, tiled=True)
@@ -737,7 +742,7 @@
     table = column_table(row_outer, row_inner, kept)
     spectra, planes, table = lax.optimization_barrier((spectra, planes, table))
     partial = column_middle(
-        spectra, table, freq_two[None, :], live_two[None, :], row_outer, row_inner
+        spectra, table, freq_two[None, :], live_two[None, :], row_outer, row_inner, tc
     )
     for part in range(1, parts):
         planes = stencil(shift_plane, height, dipole, halos, tc, False, part, parts, planes)
@@ -746,7 +751,7 @@
     for part in range(parts):
         block = lax.all_to_all(partial[part], ("tr", "tc"), split_axis=0, concat_axis=0, tiled=True)
         speed = row_inverse(block, col_outer, col_inner, tc)
-        speed = exchange(speed, part < parts - 1)
+        speed = exchange(speed)
         results = finish(speed, unit, base, part, parts, results)
     return tuple(results)
 

time: 453 us -> 481 us (1.062)
  local copies, waits for them, and re-layouts: 18.1 us -> 32.5 us
  Pallas kernels: 235 us -> 247 us
  blocking collectives: 64 us -> 52.1 us
  starting transfers between devices: 25.3 us -> 32.4 us
  waiting for transfers between devices: 107 us -> 112 us
    all_to_all x1, waiting for transfers between devices: 0.01 us -> 35.5 us  [local_kernels(): lax.all_to_all(partial[part], ('tr', 'tc'), split_axis=0, concat_axis=0,...]
    all_to_all x2 -> x4, waiting for transfers between devices: 90.4 us -> 55 us  [local_kernels(): lax.all_to_all(block, ('tr', 'tc'), split_axis=0, concat_axis=0, tiled=True)]
    all_to_all x1 -> x0, blocking collectives: 11.9 us -> none  [exchange(): return lax.all_to_all(x, 'tc', split_axis=0, concat_axis=0, tiled=True)]
    all_to_all x2 -> x4, starting transfers between devices: 10.4 us -> 20.8 us  [local_kernels(): lax.all_to_all(block, ('tr', 'tc'), split_axis=0, concat_axis=0, tiled=True)]
    pallas_call x4 -> x6, Pallas kernels: 139 us -> 146 us  [stencil(): pl.pallas_call(kernel, grid=(steps,), in_specs=pair + plane * (count - 2)...]
    unnamed x20 -> x40, local copies, waits for them, and re-layouts: 5.72 us -> 12.3 us
    dynamic_slice x2 -> x6, local copies, waits for them, and re-layouts: 4.18 us -> 10.5 us  [exchange(): sent = lax.dynamic_index_in_dim(x, other, 0, keepdims=True)]
    ppermute x2 -> x6, waiting for transfers between devices: 3.79 us -> 9.15 us  [exchange(): got = lax.ppermute(sent, 'tc', ring('tc')[0])]
  transfers between devices with their start and end apart: 10 -> 15, of which waited for: 7 -> 13; matrix products, arithmetic and copies ran while one was open for 2% -> 3% of each run, Pallas kernels for 33% -> 38%
where the time goes in v4:
time: 481 us; the launch traced here: 480 us
  Pallas kernels  247 us (51%)
  waiting for transfers between devices  112 us (23%)
  blocking collectives  52.1 us (11%)
  local copies, waits for them, and re-layouts  32.5 us (7%)
  starting transfers between devices  32.4 us (7%)
    pallas_call x6, Pallas kernels, stencil(): pl.pallas_call(kernel, grid=(steps,), in_specs=pair + plane * (count - 2)...  146 us
    all_to_all x4, waiting for transfers between devices, local_kernels(): lax.all_to_all(block, ('tr', 'tc'), split_axis=0, concat_axis=0, tiled=True)  55 us
    all_to_all x1, blocking collectives, local_kernels(): lax.all_to_all(partial[part], ('tr', 'tc'), split_axis=0, concat_axis=0,...  52.1 us
    all_to_all x1, waiting for transfers between devices, local_kernels(): lax.all_to_all(partial[part], ('tr', 'tc'), split_axis=0, concat_axis=0,...  35.5 us
    pallas_call x4, Pallas kernels, row_forward(): pl.pallas_call(kernel, grid=(2, rows // block), in_specs=[pl.BlockSpec((t...  35.1 us
    pallas_call x1, Pallas kernels, column_middle(): pl.pallas_call(kernel, out_shape=[jax.ShapeDtypeStruct((outer, 2, inner /...  33.1 us
    all_to_all x4, starting transfers between devices, local_kernels(): lax.all_to_all(block, ('tr', 'tc'), split_axis=0, concat_axis=0, tiled=True)  20.8 us
    pallas_call x2, Pallas kernels, row_inverse(): pl.pallas_call(kernel, grid=(rows // block,), in_specs=[pl.BlockSpec((out...  17.6 us
  transfers between devices with their start and end apart: 15, of which 13 were waited for; matrix products, arithmetic and copies ran while one was open for 3% of the time, Pallas kernels for 38%

profile of v4, /device:TPU:21, one launch (start us, length us, event | category | flops | bytes accessed | tf_op | source)
XLA Modules:
  0.0 479.9 jit_solution(7552981322301899007)
XLA Ops:
  7.7 6.8 %collective-permute-done.refs_9_.refs_6_ = f32[4,8,2048]{2,1,0:T(8,128)S(1)} collective-permute-done((f32[4,8,2048]{2,1,0:T(8,128)S(1)}, f32[4,8,2048]{2,1,0:T(8,128)S(1)}, u32[]{:S(2)}, u32[]{:S(2)}) %collective-permute-start) | collective-permute-done | bytes 262176 | tf_op jit(solution)/shard_map/ppermute | solution.py:700
  14.5 2.9 collective-permute-done.1.refs_10_.refs_7_
  20.0 1.5 collective-permute-done.2.refs_11_.refs_8_
  21.5 1.5 collective-permute-done.3.refs_12_.refs_9_
  24.1 16.5 %omega.4 = f32[2,2,64,2048]{3,2,1,0:T(8,128)} custom-call(f32[2,512,2048]{2,1,0:T(8,128)} %refs_2_.11, f32[2,512,2048]{2,1,0:T(8,128)} %refs_2_.11, f32[2,512,2048]{2,1,0:T(8,128)} %refs_2_.11, f32[512,2048]{1,0:T(8,128)} %refs_5_.12, f32[512,2048]{1,0:T(8,128)} %refs_5_.12, f32[512,2048]{1,0:T(8,128)} %refs_5_.12, f32[512,2048]{1,0:T(8,128)} %refs_8_.4, ...), custom_call_target="tpu_custom_call" | custom-call | tf_op jit(solution)/shard_map/omega/pallas_call | solution.py:458
  40.7 1.5 constant_dynamic-slice_fusion.5
  42.6 2.3 collective-permute-done.4
  46.4 8.7 %rows_forward.4 = f32[16,2,2,64,128]{4,3,2,1,0:T(8,128)} custom-call(f32[2,2,64,2048]{3,2,1,0:T(8,128)} %copy-done.7, f32[2,16,8,256]{3,2,1,0:T(8,128)} %broadcast_in_dim.28.tw_ref, bf16[2,512,256]{2,1,0:T(8,128)(2,1)} %constant.81.clone.m_ref), custom_call_target="tpu_custom_call" | custom-call | tf_op jit(solution)/shard_map/rows_forward/pallas_call | solution.py:520
  55.1 5.3 %all-to-all-start = ((f32[16,2,2,64,128]{4,3,2,1,0:T(8,128)}), f32[16,2,2,64,128]{4,3,2,1,0:T(8,128)S(1)}, u32[]{:S(2)}, u32[]{:S(2)}) async-start(f32[16,2,2,64,128]{4,3,2,1,0:T(8,128)} %rows_forward.4), calls=%async_computation | async-start | bytes 4194304 | tf_op jit(solution)/shard_map/all_to_all | solution.py:736
  60.4 16.5 %omega.5 = f32[2,2,64,2048]{3,2,1,0:T(8,128)} custom-call(f32[2,512,2048]{2,1,0:T(8,128)} %refs_2_.11, f32[2,512,2048]{2,1,0:T(8,128)} %refs_2_.11, f32[2,512,2048]{2,1,0:T(8,128)} %refs_2_.11, f32[512,2048]{1,0:T(8,128)} %refs_5_.12, f32[512,2048]{1,0:T(8,128)} %refs_5_.12, f32[512,2048]{1,0:T(8,128)} %refs_5_.12, f32[512,2048]{1,0:T(8,128)} %refs_8_.4, ...), custom_call_target="tpu_custom_call" | custom-call | tf_op jit(solution)/shard_map/omega/pallas_call | solution.py:458
  77.0 1.5 constant_dynamic-slice_fusion.4
  78.9 2.3 collective-permute-done.5
  81.3 1.3 copy-done.9
  82.6 8.8 %rows_forward.5 = f32[16,2,2,64,128]{4,3,2,1,0:T(8,128)} custom-call(f32[2,2,64,2048]{3,2,1,0:T(8,128)} %copy-done.9, f32[2,16,8,256]{3,2,1,0:T(8,128)} %broadcast_in_dim.28.tw_ref, bf16[2,512,256]{2,1,0:T(8,128)(2,1)} %constant.81.clone.m_ref), custom_call_target="tpu_custom_call" | custom-call | tf_op jit(solution)/shard_map/rows_forward/pallas_call | solution.py:520
  91.4 16.0 %all-to-all-done.refs_0_ = f32[16,2,2,64,128]{4,3,2,1,0:T(8,128)S(1)} async-done(((f32[16,2,2,64,128]{4,3,2,1,0:T(8,128)}), f32[16,2,2,64,128]{4,3,2,1,0:T(8,128)S(1)}, u32[]{:S(2)}, u32[]{:S(2)}) %all-to-all-start) | async-done | bytes 2097184 | tf_op jit(solution)/shard_map/all_to_all | solution.py:736
  107.5 1.3 copy-done.17
  108.8 5.2 %all-to-all-start.1 = ((f32[16,2,2,64,128]{4,3,2,1,0:T(8,128)}), f32[16,2,2,64,128]{4,3,2,1,0:T(8,128)}, u32[]{:S(2)}, u32[]{:S(2)}) async-start(f32[16,2,2,64,128]{4,3,2,1,0:T(8,128)} %rows_forward.5), calls=%async_computation.1 | async-start | bytes 4194304 | tf_op jit(solution)/shard_map/all_to_all | solution.py:736
  114.0 16.5 %omega.6 = f32[2,2,64,2048]{3,2,1,0:T(8,128)} custom-call(f32[2,512,2048]{2,1,0:T(8,128)} %refs_2_.11, f32[2,512,2048]{2,1,0:T(8,128)} %refs_2_.11, f32[2,512,2048]{2,1,0:T(8,128)} %refs_2_.11, f32[512,2048]{1,0:T(8,128)} %refs_5_.12, f32[512,2048]{1,0:T(8,128)} %refs_5_.12, f32[512,2048]{1,0:T(8,128)} %refs_5_.12, f32[512,2048]{1,0:T(8,128)} %refs_8_.4, ...), custom_call_target="tpu_custom_call" | custom-call | tf_op jit(solution)/shard_map/omega/pallas_call | solution.py:458
  130.5 1.5 constant_dynamic-slice_fusion.3
  132.4 2.3 collective-permute-done.6
  136.2 8.8 %rows_forward.6 = f32[16,2,2,64,128]{4,3,2,1,0:T(8,128)} custom-call(f32[2,2,64,2048]{3,2,1,0:T(8,128)} %copy-done.11, f32[2,16,8,256]{3,2,1,0:T(8,128)} %broadcast_in_dim.28.tw_ref, bf16[2,512,256]{2,1,0:T(8,128)(2,1)} %constant.81.clone.m_ref), custom_call_target="tpu_custom_call" | custom-call | tf_op jit(solution)/shard_map/rows_forward/pallas_call | solution.py:520
  144.9 16.2 %all-to-all-done.1.refs_1_ = f32[16,2,2,64,128]{4,3,2,1,0:T(8,128)} async-done(((f32[16,2,2,64,128]{4,3,2,1,0:T(8,128)}), f32[16,2,2,64,128]{4,3,2,1,0:T(8,128)}, u32[]{:S(2)}, u32[]{:S(2)}) %all-to-all-start.1) | async-done | bytes 2097184 | tf_op jit(solution)/shard_map/all_to_all | solution.py:736
  161.1 5.2 %all-to-all-start.2 = ((f32[16,2,2,64,128]{4,3,2,1,0:T(8,128)}), f32[16,2,2,64,128]{4,3,2,1,0:T(8,128)S(1)}, u32[]{:S(2)}, u32[]{:S(2)}) async-start(f32[16,2,2,64,128]{4,3,2,1,0:T(8,128)} %rows_forward.6), calls=%async_computation.2 | async-start | bytes 4194304 | tf_op jit(solution)/shard_map/all_to_all | solution.py:736
  166.3 16.5 %omega.7 = f32[2,2,64,2048]{3,2,1,0:T(8,128)} custom-call(f32[2,512,2048]{2,1,0:T(8,128)} %refs_2_.11, f32[2,512,2048]{2,1,0:T(8,128)} %refs_2_.11, f32[2,512,2048]{2,1,0:T(8,128)} %refs_2_.11, f32[512,2048]{1,0:T(8,128)} %refs_5_.12, f32[512,2048]{1,0:T(8,128)} %refs_5_.12, f32[512,2048]{1,0:T(8,128)} %refs_5_.12, f32[512,2048]{1,0:T(8,128)} %refs_8_.4, ...), custom_call_target="tpu_custom_call" | custom-call | tf_op jit(solution)/shard_map/omega/pallas_call | solution.py:458
  182.8 1.5 constant_dynamic-slice_fusion.2
  184.7 2.3 collective-permute-done.7
  188.5 8.8 %rows_forward.7 = f32[16,2,2,64,128]{4,3,2,1,0:T(8,128)} custom-call(f32[2,2,64,2048]{3,2,1,0:T(8,128)} %copy-done.13, f32[2,16,8,256]{3,2,1,0:T(8,128)} %broadcast_in_dim.28.tw_ref, bf16[2,512,256]{2,1,0:T(8,128)(2,1)} %constant.81.clone.m_ref), custom_call_target="tpu_custom_call" | custom-call | tf_op jit(solution)/shard_map/rows_forward/pallas_call | solution.py:520
  197.3 16.0 %all-to-all-done.2.refs_2_ = f32[16,2,2,64,128]{4,3,2,1,0:T(8,128)S(1)} async-done(((f32[16,2,2,64,128]{4,3,2,1,0:T(8,128)}), f32[16,2,2,64,128]{4,3,2,1,0:T(8,128)S(1)}, u32[]{:S(2)}, u32[]{:S(2)}) %all-to-all-start.2) | async-done | bytes 2097184 | tf_op jit(solution)/shard_map/all_to_all | solution.py:736
  213.3 1.3 copy-done.18
  214.7 5.2 %all-to-all-start.3 = ((f32[16,2,2,64,128]{4,3,2,1,0:T(8,128)}), f32[16,2,2,64,128]{4,3,2,1,0:T(8,128)}, u32[]{:S(2)}, u32[]{:S(2)}) async-start(f32[16,2,2,64,128]{4,3,2,1,0:T(8,128)} %rows_forward.7), calls=%async_computation.3 | async-start | bytes 4194304 | tf_op jit(solution)/shard_map/all_to_all | solution.py:736
  220.4 39.8 %geometry.2 = (f32[3,512,2048]{2,1,0:T(8,128)}, f32[512,2048]{1,0:T(8,128)}) custom-call(f32[2,512,2048]{2,1,0:T(8,128)} %refs_2_.11, f32[2,512,2048]{2,1,0:T(8,128)} %refs_2_.11, f32[2,512,2048]{2,1,0:T(8,128)} %refs_2_.11, f32[512,2048]{1,0:T(8,128)} %refs_5_.12, f32[512,2048]{1,0:T(8,128)} %refs_5_.12, f32[512,2048]{1,0:T(8,128)} %refs_5_.12, ...), custom_call_target="tpu_custom_call" | custom-call | tf_op jit(solution)/shard_map/geometry/pallas_call | solution.py:458
  260.2 6.8 %all-to-all-done.3.refs_3_ = f32[16,2,2,64,128]{4,3,2,1,0:T(8,128)} async-done(((f32[16,2,2,64,128]{4,3,2,1,0:T(8,128)}), f32[16,2,2,64,128]{4,3,2,1,0:T(8,128)}, u32[]{:S(2)}, u32[]{:S(2)}) %all-to-all-start.3) | async-done | bytes 2097184 | tf_op jit(solution)/shard_map/all_to_all | solution.py:736
  267.0 2.6 broadcast_in_dim.32.refs_4_
  269.6 33.1 %columns.1 = (f32[16,2,128,128]{3,2,1,0:T(8,128)}, f32[16,2,128,128]{3,2,1,0:T(8,128)}) custom-call(f32[16,2,2,64,128]{4,3,2,1,0:T(8,128)} %copy-done.17, f32[16,2,2,64,128]{4,3,2,1,0:T(8,128)} %all-to-all-done.1.refs_1_, f32[16,2,2,64,128]{4,3,2,1,0:T(8,128)} %copy-done.18, f32[16,2,2,64,128]{4,3,2,1,0:T(8,128)} %all-to-all-done.3.refs_3_, ...), custom_call_target="tpu_custom_call" | custom-call | tf_op jit(solution)/shard_map/columns/pallas_call | solution.py:624
  302.7 52.1 %all_to_all.30.x_ref = f32[16,2,128,128]{3,2,1,0:T(8,128)} all-to-all(f32[16,2,128,128]{3,2,1,0:T(8,128)} %get-tuple-element.43), channel_id=1, replica_groups=mesh['groups'=2,'tr'=8,'tc'=2] {'tr','tc'}, dimensions={0} | all-to-all | bytes 4194304 | tf_op jit(solution)/shard_map/all_to_all | solution.py:752
  354.8 5.5 %all-to-all-start.4 = ((f32[16,2,128,128]{3,2,1,0:T(8,128)}), f32[16,2,128,128]{3,2,1,0:T(8,128)S(1)}, u32[]{:S(2)}, u32[]{:S(2)}) async-start(f32[16,2,128,128]{3,2,1,0:T(8,128)} %get-tuple-element.38), calls=%async_computation.4 | async-start | bytes 4194304 | tf_op jit(solution)/shard_map/all_to_all | solution.py:752
  360.3 8.8 %rows_inverse.3 = f32[2,128,2048]{2,1,0:T(8,128)} custom-call(f32[16,2,128,128]{3,2,1,0:T(8,128)} %all_to_all.30.x_ref, f32[2,16,8,256]{3,2,1,0:T(8,128)} %broadcast_in_dim.28.tw_ref, bf16[2,256,512]{2,1,0:T(8,128)(2,1)} %constant.83.clone.m_ref), custom_call_target="tpu_custom_call" | custom-call | tf_op jit(solution)/shard_map/rows_inverse/pallas_call | solution.py:675
  369.1 2.3 constant_dynamic-slice_fusion
  371.8 35.5 %all-to-all-done.4.x_ref = f32[16,2,128,128]{3,2,1,0:T(8,128)S(1)} async-done(((f32[16,2,128,128]{3,2,1,0:T(8,128)}), f32[16,2,128,128]{3,2,1,0:T(8,128)S(1)}, u32[]{:S(2)}, u32[]{:S(2)}) %all-to-all-start.4) | async-done | bytes 2097184 | tf_op jit(solution)/shard_map/all_to_all | solution.py:752
  407.3 1.3 copy-done.16
  408.7 8.8 %rows_inverse.2 = f32[2,128,2048]{2,1,0:T(8,128)} custom-call(f32[16,2,128,128]{3,2,1,0:T(8,128)} %copy-done.16, f32[2,16,8,256]{3,2,1,0:T(8,128)} %broadcast_in_dim.28.tw_ref, bf16[2,256,512]{2,1,0:T(8,128)(2,1)} %constant.83.clone.m_ref), custom_call_target="tpu_custom_call" | custom-call | tf_op jit(solution)/shard_map/rows_inverse/pallas_call | solution.py:675
  417.5 2.3 constant_dynamic-slice_fusion.1
  420.8 39.8 %geometry.3 = (f32[3,512,2048]{2,1,0:T(8,128)}, f32[512,2048]{1,0:T(8,128)}) custom-call(f32[2,512,2048]{2,1,0:T(8,128)} %refs_2_.11, f32[2,512,2048]{2,1,0:T(8,128)} %refs_2_.11, f32[2,512,2048]{2,1,0:T(8,128)} %refs_2_.11, f32[512,2048]{1,0:T(8,128)} %refs_5_.12, f32[512,2048]{1,0:T(8,128)} %refs_5_.12, ...), custom_call_target="tpu_custom_call", output_to_operand_aliasing={{0}: (10, {}), {1}: (11, {})} | custom-call | tf_op jit(solution)/shard_map/geometry/pallas_call | solution.py:458
  460.7 1.3 copy-done.5
  462.1 7.7 %finish.2 = (f32[3,512,2048]{2,1,0:T(8,128)}, f32[512,2048]{1,0:T(8,128)}) custom-call(f32[2,128,2048]{2,1,0:T(8,128)} %copy-done.5, f32[3,512,2048]{2,1,0:T(8,128)} %get-tuple-element.41.u_ref, f32[512,2048]{1,0:T(8,128)} %get-tuple-element.42.b_ref), custom_call_target="tpu_custom_call" | custom-call | tf_op jit(solution)/shard_map/finish/pallas_call | solution.py:775
  469.7 1.3 constant_dynamic-update-slice_fusion.1.s_ref
  471.1 1.3 copy-done.3
  472.4 7.5 %finish.3 = (f32[3,512,2048]{2,1,0:T(8,128)}, f32[512,2048]{1,0:T(8,128)}) custom-call(f32[2,128,2048]{2,1,0:T(8,128)} %copy-done.3, f32[3,512,2048]{2,1,0:T(8,128)} %get-tuple-element.41.u_ref, f32[512,2048]{1,0:T(8,128)} %get-tuple-element.42.b_ref, f32[3,512,2048]{2,1,0:T(8,128)} %get-tuple-element.44.refs_0_, ...), custom_call_target="tpu_custom_call", output_to_operand_aliasing={{0}: (3, {}), {1}: (4, {})} | custom-call | tf_op jit(solution)/shard_map/finish/pallas_call | solution.py:775
  (63 shorter events, 19.0 us)
Async XLA Ops:
  2.6 11.9 %collective-permute-start = (f32[4,8,2048]{2,1,0:T(8,128)S(1)}, f32[4,8,2048]{2,1,0:T(8,128)S(1)}, u32[]{:S(2)}, u32[]{:S(2)}) collective-permute-start(f32[4,8,2048]{2,1,0:T(8,128)S(1)} %pad_maximum_fusion.2), channel_id=1, source_target_pairs={{0,2},{2,4},{4,6},{6,8},{8,10},{10,12},{12,14},{14,0},{1,3},{3,5},... | collective-permute-start | bytes 786440 | tf_op jit(solution)/shard_map/ppermute | solution.py:700
  3.9 13.5 %collective-permute-start.1 = (f32[4,8,2048]{2,1,0:T(8,128)S(1)}, f32[4,8,2048]{2,1,0:T(8,128)S(1)}, u32[]{:S(2)}, u32[]{:S(2)}) collective-permute-start(f32[4,8,2048]{2,1,0:T(8,128)S(1)} %pad_maximum_fusion.3), channel_id=1, source_target_pairs={{2,0},{4,2},{6,4},{8,6},{10,8},{12,10},{14,12},{0,14},{3,1},{5,3},... | collective-permute-start | bytes 786440 | tf_op jit(solution)/shard_map/ppermute | solution.py:701
  14.5 5.5 %copy-start.14 = (f32[4,8,2048]{2,1,0:T(8,128)}, f32[4,8,2048]{2,1,0:T(8,128)S(1)}, u32[]{:S(2)}) copy-start(f32[4,8,2048]{2,1,0:T(8,128)S(1)} %collective-permute-done.refs_9_.refs_6_) | copy-start | bytes 786436
  17.4 2.6 copy-start.15
  18.5 3.0 collective-permute-start.2
  20.0 3.0 collective-permute-start.3
  21.5 1.5 copy-start
  23.1 1.1 copy-start.1
  40.6 4.2 copy-start.6
  40.7 4.3 copy-start.19
  42.1 2.7 collective-permute-start.4
  45.0 1.4 copy-start.7
  55.1 52.4 %all-to-all-start = ((f32[16,2,2,64,128]{4,3,2,1,0:T(8,128)}), f32[16,2,2,64,128]{4,3,2,1,0:T(8,128)S(1)}, u32[]{:S(2)}, u32[]{:S(2)}) async-start(f32[16,2,2,64,128]{4,3,2,1,0:T(8,128)} %rows_forward.4), calls=%async_computation | async-start | bytes 4194304 | tf_op jit(solution)/shard_map/all_to_all | solution.py:736
  77.0 4.2 copy-start.8
  78.5 2.7 collective-permute-start.5
  81.3 1.3 copy-start.9
  107.5 1.3 copy-start.17
  108.8 52.3 %all-to-all-start.1 = ((f32[16,2,2,64,128]{4,3,2,1,0:T(8,128)}), f32[16,2,2,64,128]{4,3,2,1,0:T(8,128)}, u32[]{:S(2)}, u32[]{:S(2)}) async-start(f32[16,2,2,64,128]{4,3,2,1,0:T(8,128)} %rows_forward.5), calls=%async_computation.1 | async-start | bytes 4194304 | tf_op jit(solution)/shard_map/all_to_all | solution.py:736
  130.5 4.2 copy-start.10
  132.0 2.7 collective-permute-start.6
  134.8 1.3 copy-start.11
  161.1 52.2 %all-to-all-start.2 = ((f32[16,2,2,64,128]{4,3,2,1,0:T(8,128)}), f32[16,2,2,64,128]{4,3,2,1,0:T(8,128)S(1)}, u32[]{:S(2)}, u32[]{:S(2)}) async-start(f32[16,2,2,64,128]{4,3,2,1,0:T(8,128)} %rows_forward.6), calls=%async_computation.2 | async-start | bytes 4194304 | tf_op jit(solution)/shard_map/all_to_all | solution.py:736
  182.8 4.2 copy-start.12
  184.3 2.7 collective-permute-start.7
  187.1 1.3 copy-start.13
  213.3 1.4 copy-start.18
  214.7 52.3 %all-to-all-start.3 = ((f32[16,2,2,64,128]{4,3,2,1,0:T(8,128)}), f32[16,2,2,64,128]{4,3,2,1,0:T(8,128)}, u32[]{:S(2)}, u32[]{:S(2)}) async-start(f32[16,2,2,64,128]{4,3,2,1,0:T(8,128)} %rows_forward.7), calls=%async_computation.3 | async-start | bytes 4194304 | tf_op jit(solution)/shard_map/all_to_all | solution.py:736
  354.8 52.5 %all-to-all-start.4 = ((f32[16,2,128,128]{3,2,1,0:T(8,128)}), f32[16,2,128,128]{3,2,1,0:T(8,128)S(1)}, u32[]{:S(2)}, u32[]{:S(2)}) async-start(f32[16,2,128,128]{3,2,1,0:T(8,128)} %get-tuple-element.38), calls=%async_computation.4 | async-start | bytes 4194304 | tf_op jit(solution)/shard_map/all_to_all | solution.py:752
  371.4 89.2 %collective-permute-start.9 = (f32[1,128,2048]{2,1,0:T(8,128)}, f32[1,128,2048]{2,1,0:T(8,128)S(1)}, u32[]{:S(2)}, u32[]{:S(2)}) collective-permute-start(f32[1,128,2048]{2,1,0:T(8,128)} %constant_dynamic-slice_fusion), channel_id=1, source_target_pairs={{0,1},{1,0},{2,3},{3,2},{4,5},{5,4},{6,7},{7,6},{8,9},{9,8},{10,11... | collective-permute-start | bytes 3145736 | tf_op jit(solution)/shard_map/ppermute | solution.py:716
  407.3 1.3 copy-start.16
  419.8 40.8 %copy-start.4 = (f32[2,128,2048]{2,1,0:T(8,128)S(1)}, f32[2,128,2048]{2,1,0:T(8,128)}, u32[]{:S(2)}) copy-start(f32[2,128,2048]{2,1,0:T(8,128)} %rows_inverse.3) | copy-start | bytes 6291460
  419.8 49.9 %collective-permute-start.8 = (f32[1,128,2048]{2,1,0:T(8,128)}, f32[1,128,2048]{2,1,0:T(8,128)}, u32[]{:S(2)}, u32[]{:S(2)}) collective-permute-start(f32[1,128,2048]{2,1,0:T(8,128)} %constant_dynamic-slice_fusion.1), channel_id=1, source_target_pairs={{0,1},{1,0},{2,3},{3,2},{4,5},{5,4},{6,7},{7,6},{8,9},{9,8},{10,11... | collective-permute-start | bytes 3145736 | tf_op jit(solution)/shard_map/ppermute | solution.py:716
  460.7 1.3 copy-start.5
  462.1 7.7 %copy-start.2 = (f32[2,128,2048]{2,1,0:T(8,128)S(1)}, f32[2,128,2048]{2,1,0:T(8,128)}, u32[]{:S(2)}) copy-start(f32[2,128,2048]{2,1,0:T(8,128)} %rows_inverse.2) | copy-start | bytes 6291460
  471.1 1.3 copy-start.3
